TPU v7x, 512 devices: a whole 4x4x16 slice. The times are simulated.
512 devices in a mesh: row: 64 (over x, z), col: 8 (over y, core).
Axes of the slice: x: 4, y: 4, z: 16, core: 2. Of those that a mesh axis runs over, the one named last changes fastest.
Arguments:
- pending: bfloat16 [65536, 8, 1024], P('row', 'col'), may hold values from -5 to 5
- panel: bfloat16 [65536, 2, 1024], P('row', None, 'col'), may hold values from -0.1875 to 0.1875
- panel_scale: float32 [65536, 2], P('row'), may hold values from 0.1 to 1
- inverse_blocks: bfloat16 [2, 1024, 1024], P(None, 'col'), as said below
Outputs:
- remaining: bfloat16 [65536, 8, 1024], P('row', 'col')
- solved: bfloat16 [2, 1024, 1024], P(None, 'col')
Inputs may be any that keep to these rules, and one draw needn't show every extreme that they name: `inverse_blocks`: each block is lower triangular with a positive diagonal, the inverse of a diagonal block of a Cholesky factor.
All inputs are finite; a program needn't handle non-finite values.
Results may differ from a plain program's by a relative error of at most 0.023.
Values may be sent and summed in bfloat16 or wider, within the bound.
A program may use at most 64 MiB of HBM per device.

v0:
```python
import jax
import jax.numpy as jnp
from jax import lax
from jax.sharding import PartitionSpec as P


def spread(shard, axis, root):
    mine = lax.axis_index(axis) == root
    return lax.psum(jnp.where(mine, shard, jnp.zeros_like(shard)), axis)


def body(pending, panel, panel_scale, inverse_blocks):
    row_index = lax.axis_index("row")
    n_row = lax.axis_size("row")
    block = inverse_blocks.shape[2]
    total = pending.shape[0]
    current = pending[:, 0, :]
    slot_of_row = lax.broadcasted_iota(jnp.int32, (total,), 0) // block
    global_ids = slot_of_row * n_row + row_index
    solved_list = []
    for k in range(2):
        head = current.astype(jnp.float32)
        fan = lax.psum(head.astype(jnp.bfloat16), "col")
        local = jnp.dot(inverse_blocks[k], fan, preferred_element_type=jnp.float32).astype(
            jnp.bfloat16
        )
        arrived = spread(local, "row", k)
        solved_list.append(arrived)
        term = jnp.dot(panel[:, k, :], arrived, preferred_element_type=jnp.float32)
        newer = (current.astype(jnp.float32) - panel_scale[:, k : k + 1] * term).astype(
            jnp.bfloat16
        )
        current = jnp.where((global_ids > k)[:, None], newer, current)
    return (current[:, None, :], jnp.stack(solved_list))


def solution(mesh):
    placed = (P("row", "col", None), P("row", None, "col"), P("row", None), P(None, "col", None))
    return jax.shard_map(
        body,
        mesh=mesh,
        in_specs=placed,
        out_specs=(P("row", "col", None), P(None, "col", None)),
        check_vma=False,
    )
```

profile of v0, /device:TPU:8, one launch (start us, length us, event | category | flops | bytes accessed | tf_op | source)
XLA Modules:
  0.0 722.6 jit_solution(12241897476524964744)
XLA Ops:
  7.2 0.0 all-reduce.5.cloned.1.call-start
  7.2 3.9 copy.9
  11.2 0.0 copy-start.7
  11.2 0.0 copy-start.5
  11.2 0.0 copy-start.2
  11.2 0.0 all-reduce.5.cloned.1.call-update
  11.2 0.0 all-reduce.7.cloned.1.call-start
  11.3 0.6 copy-done.7
  11.9 0.0 copy-start
  11.9 82.6 %all-reduce.5.cloned.1.call-done = bf16[1024,1024]{0,1:T(8,128)(2,1)} async-done(((bf16[1024,1024]{0,1:T(8,128)(2,1)}), bf16[1024,1024]{0,1:T(8,128)(2,1)}) %all-reduce.5.cloned.1.call-update) | async-done | bytes 2097168 | tf_op jit(solution)/shard_map/psum | solution.py:23
  94.5 0.0 copy-done.5
  94.5 3.1 fusion.5
  97.6 0.0 all-reduce.7.cloned.1.call-update
  97.6 0.0 all-reduce.9.cloned.1.call-start
  97.7 0.0 copy-done.2
  97.7 1.5 fusion.19
  99.2 263.4 %all-reduce.7.cloned.1.call-done = bf16[128,1024]{1,0:T(8,128)(2,1)} async-done(((bf16[128,1024]{1,0:T(8,128)(2,1)}), bf16[128,1024]{1,0:T(8,128)(2,1)}) %all-reduce.7.cloned.1.call-update) | async-done | bytes 262160 | tf_op jit(solution)/shard_map/psum | solution.py:9
  362.6 0.0 copy-done
  362.6 3.3 fusion.2
  365.9 0.0 copy-start.6
  365.9 0.0 all-reduce.9.cloned.1.call-update
  365.9 0.0 copy-start.1
  365.9 0.0 all-reduce.11.cloned.1.call-start
  366.0 73.2 %all-reduce.9.cloned.1.call-done = bf16[1024,1024]{0,1:T(8,128)(2,1)} async-done(((bf16[1024,1024]{0,1:T(8,128)(2,1)}), bf16[1024,1024]{0,1:T(8,128)(2,1)}) %all-reduce.9.cloned.1.call-update) | async-done | bytes 2097168 | tf_op jit(solution)/shard_map/psum | solution.py:23
  439.2 0.0 copy-done.6
  439.2 3.1 fusion.7
  442.3 0.0 all-reduce.11.cloned.1.call-update
  442.4 265.7 %all-reduce.11.cloned.1.call-done = bf16[128,1024]{1,0:T(8,128)(2,1)} async-done(((bf16[128,1024]{1,0:T(8,128)(2,1)}), bf16[128,1024]{1,0:T(8,128)(2,1)}) %all-reduce.11.cloned.1.call-update) | async-done | bytes 262160 | tf_op jit(solution)/shard_map/psum | solution.py:9
  708.1 0.0 copy-done.1
  708.1 3.1 fusion.4
  711.3 0.0 copy-start.3
  711.3 0.0 copy-start.4
  711.3 4.0 copy.13
  715.3 0.0 copy-done.3
  715.3 0.0 copy-done.4
  715.3 0.8 pad_maximum_fusion
  (3 shorter events, 0.0 us)
Async XLA Ops:
  7.2 87.3 %all-reduce.5.cloned.1.call-start = ((), (), s32[]{:S(2)}) async-start(), calls=%async_computation | async-start | bytes 4194304 | tf_op jit(solution)/shard_map/psum | solution.py:23
  11.2 0.7 copy-start.7
  11.2 83.3 %copy-start.5 = (bf16[2,128,1024]{2,1,0:T(8,128)(2,1)S(1)}, bf16[2,128,1024]{2,1,0:T(8,128)(2,1)}, u32[]{:S(2)}) copy-start(bf16[2,128,1024]{2,1,0:T(8,128)(2,1)} %param.7) | copy-start | bytes 1572868
  11.2 86.5 %copy-start.2 = (bf16[1024,2,128]{2,1,0:T(2,128)(2,1)S(1)}, bf16[1024,2,128]{2,1,0:T(2,128)(2,1)}, u32[]{:S(2)}) copy-start(bf16[1024,2,128]{2,1,0:T(2,128)(2,1)} %param.5) | copy-start | bytes 1572868
  11.2 351.4 %all-reduce.7.cloned.1.call-start = ((), (), s32[]{:S(2)}) async-start(), calls=%async_computation.1 | async-start | bytes 524288 | tf_op jit(solution)/shard_map/psum | solution.py:9
  11.9 350.7 %copy-start = (bf16[1024,1,1024]{0,2,1:T(8,128)(2,1)S(1)}, bf16[1024,1,1024]{0,2,1:T(8,128)(2,1)}, u32[]{:S(2)}) copy-start(bf16[1024,1,1024]{0,2,1:T(8,128)(2,1)} %copy.9) | copy-start | bytes 6291460
  97.6 341.6 %all-reduce.9.cloned.1.call-start = ((), (), s32[]{:S(2)}) async-start(), calls=%async_computation.2 | async-start | bytes 4194304 | tf_op jit(solution)/shard_map/psum | solution.py:23
  365.9 73.3 %copy-start.6 = (bf16[2,128,1024]{2,1,0:T(8,128)(2,1)S(1)}, bf16[2,128,1024]{2,1,0:T(8,128)(2,1)}, u32[]{:S(2)}) copy-start(bf16[2,128,1024]{2,1,0:T(8,128)(2,1)} %param.7) | copy-start | bytes 1572868
  365.9 342.2 %copy-start.1 = (bf16[1024,1024]{0,1:T(8,128)(2,1)S(1)}, bf16[1024,1024]{0,1:T(8,128)(2,1)}, u32[]{:S(2)}) copy-start(bf16[1024,1024]{0,1:T(8,128)(2,1)} %fusion.2) | copy-start | bytes 6291460
  365.9 342.2 %all-reduce.11.cloned.1.call-start = ((), (), s32[]{:S(2)}) async-start(), calls=%async_computation.3 | async-start | bytes 524288 | tf_op jit(solution)/shard_map/psum | solution.py:9
  711.3 4.0 copy-start.3
  711.3 4.0 copy-start.4
Sparse Core Ops, SparseCore 0:
  11.3 83.1 all-reduce.4
  97.9 264.6 all-reduce.6
  366.0 73.1 all-reduce.8
  443.5 264.6 all-reduce.10
where the time goes:
time: 723 us
  waiting for transfers between devices  685 us (95%)
  between operations  13.8 us (2%)
  matrix products  12.7 us (2%)
  local copies, waits for them, and re-layouts  10.1 us (1%)
    psum x2, waiting for transfers between devices, spread(): return lax.psum(jnp.where(mine, shard, jnp.zeros_like(shard)), axis)  529 us
    psum x2, waiting for transfers between devices, body(): fan = lax.psum(head.astype(jnp.bfloat16), 'col')  156 us
  transfers between devices with their start and end apart: 4, of which 4 were waited for; matrix products, arithmetic and copies ran while one was open for 0% of the time, Pallas kernels for 0%

commit v1 on v0

v1 whole, which is shorter than its diff:
```python
import functools

import jax
import jax.numpy as jnp
from jax import lax
from jax.experimental import pallas as pl
from jax.experimental.pallas import tpu as pltpu
from jax.sharding import PartitionSpec as P

MESH = pl.DeviceIdType.MESH
NX, NY, NZ = 4, 4, 16
BF = jnp.bfloat16
F32 = jnp.float32
FAR_FIRST = (8, 9, 7, 10, 6, 11, 5, 12, 4, 13, 3, 14, 2, 15, 1)


def comm_kernel(
    pend, scaled, linv, out,
    cur, xin, part, fan, linv_o, oblk, pmat,
    ld, xs, xr, ps, pr, as_, ar, ls, lr, zs, zr_, fs, fr,
):
    row, col = lax.axis_index("row"), lax.axis_index("col")
    x, z = row // NZ, row % NZ
    y, h = col // 2, col % 2
    other = 2 * y + (1 - h)
    even = x % 2 == 0

    def zrel(k):
        return (z - k + NZ) % NZ

    def lead_z(k):
        zr = zrel(k)
        second = jnp.where(even, 1, NZ - 1)
        return jnp.logical_or(zr == 0, zr == second)

    mine = h == x // 2
    second = jnp.where(even, 1, NZ - 1)

    def dev(xx, zz, cc):
        return (xx * NZ + zz, cc)

    source = [jnp.logical_and(x == 0, z == k) for k in range(2)]
    is_source = jnp.logical_or(source[0], source[1])

    @pl.when(is_source)
    def _():
        pltpu.make_async_copy(pend, cur, ld.at[0]).start()

    @pl.when(source[1])
    def _():
        pltpu.make_async_copy(scaled.at[:, pl.ds(0, 128)], pmat, ld.at[1]).start()

    bar = pltpu.get_barrier_semaphore()

    def hello(target):
        pl.semaphore_signal(bar, inc=1, device_id=target, device_id_type=MESH)

    hello((row, other))
    for d in range(1, NX):
        hello(dev((x + d) % NX, z, col))
    lead_col = 2 * y + x // 2
    expect = jnp.int32(1 + NX - 1)
    for k in range(2):
        for j in range(2):
            lz = (k + (0 if j == 0 else second)) % NZ
            @pl.when(z != lz)
            def _():
                hello(dev(x, lz, lead_col))
        lead = jnp.logical_and(lead_z(k), mine)
        for yd in range(1, NY):
            @pl.when(lead)
            def _():
                hello((row, 2 * ((y + yd) % NY) + h))
        for yd in range(NY):
            sy = (y + yd) % NY
            @pl.when(jnp.logical_and(lead, jnp.logical_or(jnp.logical_not(source[k]), sy != y)))
            def _():
                hello((k, 2 * sy + h))
        expect += jnp.where(lead, 2 * (NZ - 1) + NY - 1, 0)
        expect += jnp.where(source[k], jnp.where(h == 0, 4 * NY - 1, 4 * NY), 0)
    pl.semaphore_wait(bar, expect)

    def linv_copy(k):
        return pltpu.make_async_remote_copy(
            linv.at[k], linv_o.at[k], ls.at[k], lr.at[k], device_id=(row, other), device_id_type=MESH)

    gives = [jnp.logical_and(lead_z(k), jnp.logical_not(mine)) for k in range(2)]

    def half(i):
        return pl.ds(pl.multiple_of((4 * (1 - h) + i) * 128, 128), 128)

    def own(i):
        return pl.ds(pl.multiple_of((4 * h + i) * 128, 128), 128)

    def swap_copy(i):
        return pltpu.make_async_remote_copy(
            cur.at[:, half(i)], xin.at[i], xs.at[i], xr.at[i], device_id=(row, other), device_id_type=MESH)

    def scatter_copy(k, i, yd):
        zoff = 0 if i % 2 == 0 else (1 if i // 2 == 0 else NZ - 1)
        ty = (y + yd) % NY
        rows = pl.ds(pl.multiple_of(ty * 256, 256), 256)
        return pltpu.make_async_remote_copy(
            xin.at[i, rows], part.at[k, yd], ps.at[i, yd], pr.at[k, yd],
            device_id=dev(2 * h + i // 2, (k + zoff) % NZ, 2 * ty + h), device_id_type=MESH)

    def add_and_scatter(k):
        for i in range(4):
            swap_copy(i).wait_recv()

            def add(r, c):
                rows = pl.ds(pl.multiple_of(r * 256, 256), 256)
                xin[i, rows] = (cur[rows, own(i)].astype(F32) + xin[i, rows].astype(F32)).astype(BF)
                return c
            lax.fori_loop(0, 4, add, 0)
            for yd in range(NY):
                if i == 0 and yd == 0:
                    @pl.when(h == 0)
                    def _():
                        part[k, 0] = xin[0, pl.ds(pl.multiple_of(y * 256, 256), 256)]

                    @pl.when(h != 0)
                    def _():
                        scatter_copy(k, i, yd).start()
                else:
                    scatter_copy(k, i, yd).start()

    def gather_copy(k, yd):
        rows = pl.ds(pl.multiple_of(y * 256, 256), 256)
        return pltpu.make_async_remote_copy(
            fan.at[k, rows], fan.at[k, rows], as_.at[k, yd - 1], ar.at[k, yd - 1],
            device_id=(row, 2 * ((y + yd) % NY) + h), device_id_type=MESH)

    def piece(k, xx, j):
        return out.at[k, :, pl.ds(pl.multiple_of((2 * xx + j) * 128, 128), 128)]

    def my_j(k):
        return jnp.where(zrel(k) == 0, 0, 1)

    def line_copy(k, j, d, same):
        target = dev(x, (z + d) % NZ, col if same else other)
        src = piece(k, x, j) if same else oblk.at[k]
        return pltpu.make_async_remote_copy(
            src, piece(k, x, j), zs.at[k, d, 0 if same else 1], zr_.at[k, j],
            device_id=target, device_id_type=MESH)

    def lead_step(k):
        for yd in range(NY):
            if yd == 0:
                @pl.when(jnp.logical_not(source[k]))
                def _():
                    scatter_copy(k, 0, yd).wait_recv()
            else:
                scatter_copy(k, 0, yd).wait_recv()
        total = part[k, 0].astype(F32)
        for yd in range(1, NY):
            total += part[k, yd].astype(F32)
        fan[k, pl.ds(pl.multiple_of(y * 256, 256), 256)] = total.astype(BF)
        for yd in range(1, NY):
            gather_copy(k, yd).start()
        linv_copy(k).wait_recv()
        for yd in range(1, NY):
            gather_copy(k, yd).wait_recv()
        f = fan[k]
        oblk[k] = jnp.dot(linv_o[k], f, preferred_element_type=F32).astype(BF)
        block = jnp.dot(linv[k], f, preferred_element_type=F32).astype(BF)
        for j in range(2):
            @pl.when(my_j(k) == j)
            def _():
                out[k, :, pl.ds(pl.multiple_of((2 * x + j) * 128, 128), 128)] = block
                for d in FAR_FIRST:
                    line_copy(k, j, d, False).start()
                    line_copy(k, j, d, True).start()
                line_copy(k, j, 0, False).start()

    def spread_copy(k, j, d):
        tx = (x + d) % NX
        return pltpu.make_async_remote_copy(
            piece(k, x, j), piece(k, x, j), fs.at[k, j, d - 1], fr.at[k, j, d - 1],
            device_id=dev(tx, z, col), device_id_type=MESH)

    def spread_wait(k, j, d):
        fx = (x + NX - d) % NX
        return pltpu.make_async_remote_copy(
            piece(k, fx, j), piece(k, fx, j), fs.at[k, j, d - 1], fr.at[k, j, d - 1],
            device_id=dev(fx, z, col), device_id_type=MESH)

    for k in range(2):
        @pl.when(gives[k])
        def _():
            linv_copy(k).start()

    for k in range(2):
        @pl.when(source[k])
        def _():
            if k == 0:
                pltpu.make_async_copy(pend, cur, ld.at[0]).wait()
                for i in range(4):
                    swap_copy(i).start()
            else:
                for j in range(2):
                    for d in range(1, NX):
                        spread_wait(0, j, d).wait_recv()
                pltpu.make_async_copy(pend, cur, ld.at[0]).wait()
                pltpu.make_async_copy(scaled.at[:, pl.ds(0, 128)], pmat, ld.at[1]).wait()

                def update(cols):
                    def tile(r, c):
                        rows = pl.ds(pl.multiple_of(r * 256, 256), 256)
                        term = jnp.dot(pmat[rows], out[0, :, cols], preferred_element_type=F32)
                        cur[rows, cols] = (cur[rows, cols].astype(F32) - term).astype(BF)
                        return c
                    lax.fori_loop(0, 4, tile, 0)
                for i in range(4):
                    update(half(i))
                    swap_copy(i).start()
                for i in range(4):
                    update(own(i))
            add_and_scatter(k)

        lead = jnp.logical_and(lead_z(k), mine)

        @pl.when(lead)
        def _():
            lead_step(k)

        for j in range(2):
            @pl.when(jnp.logical_not(jnp.logical_and(lead, my_j(k) == j)))
            def _():
                line_copy(k, j, 0, False).wait_recv()
            for d in (2, 1, 3):
                spread_copy(k, j, d).start()

    for k in range(2):
        for j in range(2):
            for d in range(1, NX):
                if k == 0:
                    @pl.when(jnp.logical_not(source[1]))
                    def _():
                        spread_wait(k, j, d).wait_recv()
                else:
                    spread_wait(k, j, d).wait_recv()
                spread_copy(k, j, d).wait_send()

    for k in range(2):
        @pl.when(gives[k])
        def _():
            linv_copy(k).wait_send()

        @pl.when(source[k])
        def _():
            for i in range(4):
                swap_copy(i).wait_send()
                for yd in range(NY):
                    if i == 0 and yd == 0:
                        @pl.when(h != 0)
                        def _():
                            scatter_copy(k, i, yd).wait_send()
                    else:
                        scatter_copy(k, i, yd).wait_send()

        @pl.when(jnp.logical_and(lead_z(k), mine))
        def _():
            for yd in range(1, NY):
                gather_copy(k, yd).wait_send()
            for d in FAR_FIRST:
                line_copy(k, 0, d, False).wait_send()
                line_copy(k, 0, d, True).wait_send()
            line_copy(k, 0, 0, False).wait_send()


def update_kernel(pend, scaled, solved, out):
    for c in range(4):
        cols = slice(c * 256, (c + 1) * 256)
        term = jnp.dot(scaled[...], solved[:, cols], preferred_element_type=F32)
        out[:, cols] = (pend[:, cols].astype(F32) - term).astype(BF)


def body(pending, panel, panel_scale, inverse_blocks):
    row = lax.axis_index("row")
    rows, _, cols = pending.shape
    current = pending.reshape(rows, cols)
    active = (row > jnp.arange(2)).astype(F32)
    scaled = (panel.astype(F32) * (panel_scale * active)[:, :, None]).astype(BF).reshape(rows, 256)
    anyspec = pl.BlockSpec(memory_space=pl.ANY)
    vmem = pl.BlockSpec(memory_space=pltpu.VMEM)
    dma = pltpu.SemaphoreType.DMA
    solved = pl.pallas_call(
        comm_kernel,
        out_shape=jax.ShapeDtypeStruct((2, 128, cols), BF),
        in_specs=[anyspec, anyspec, vmem],
        out_specs=vmem,
        scratch_shapes=[
            pltpu.VMEM((rows, cols), BF),
            pltpu.VMEM((4, rows, 128), BF),
            pltpu.VMEM((2, NY, 256, 128), BF),
            pltpu.VMEM((2, rows, 128), BF),
            pltpu.VMEM((2, 128, cols), BF),
            pltpu.VMEM((2, 128, 128), BF),
            pltpu.VMEM((rows, 128), BF),
            dma((2,)), dma((4,)), dma((4,)), dma((4, NY)), dma((2, NY)),
            dma((2, NY - 1)), dma((2, NY - 1)), dma((2,)), dma((2,)),
            dma((2, NZ, 2)), dma((2, 2)), dma((2, 2, NX - 1)), dma((2, 2, NX - 1)),
        ],
        compiler_params=pltpu.CompilerParams(
            collective_id=0, has_side_effects=True, vmem_limit_bytes=32 << 20),
        name="substitute",
    )(current, scaled, inverse_blocks)
    tile = 256
    remaining = pl.pallas_call(
        update_kernel,
        grid=(rows // tile,),
        out_shape=jax.ShapeDtypeStruct((rows, cols), BF),
        in_specs=[
            pl.BlockSpec((tile, cols), lambda i: (i, 0)),
            pl.BlockSpec((tile, 256), lambda i: (i, 0)),
            pl.BlockSpec((256, cols), lambda i: (0, 0)),
        ],
        out_specs=pl.BlockSpec((tile, cols), lambda i: (i, 0)),
        compiler_params=pltpu.CompilerParams(vmem_limit_bytes=32 << 20),
        name="update",
    )(current, scaled, solved.reshape(256, cols))
    return remaining[:, None, :], solved


def solution(mesh):
    placed = (P("row", "col", None), P("row", None, "col"), P("row", None), P(None, "col", None))
    return jax.shard_map(
        body,
        mesh=mesh,
        in_specs=placed,
        out_specs=(P("row", "col", None), P(None, "col", None)),
        check_vma=False,
    )
```

time: 723 us -> 89 us (0.12)
  the two profiles are of different devices: /device:TPU:8 before, /device:TPU:64 now
where the time goes in v1:
time: 89 us; the launch traced here: 88.8 us
  Pallas kernels  82.6 us (93%)
  other arithmetic  4.38 us (5%)
  local copies, waits for them, and re-layouts  1.11 us (1%)
    pallas_call x1, Pallas kernels, body(): pl.pallas_call(comm_kernel, out_shape=jax.ShapeDtypeStruct((2, 128, cols)...  80.1 us
    convert_element_type x1, other arithmetic, body(): (panel.astype(F32) * (panel_scale * active)[:, :, None]).astype(BF)  3.45 us
    pallas_call x1, Pallas kernels, body(): pl.pallas_call(update_kernel, grid=(rows // tile,), out_shape=jax.ShapeDt...  2.53 us

profile of v1, /device:TPU:64, one launch (start us, length us, event | category | flops | bytes accessed | tf_op | source)
XLA Modules:
  0.0 88.8 jit_solution(4943842807088819744)
XLA Ops:
  0.6 0.0 copy-start
  0.6 0.0 copy-start.1
  0.7 0.9 %broadcast_multiply_fusion = f32[1024,2]{0,1:T(2,128)S(1)} fusion(f32[1024,2]{0,1:T(2,128)} %param.6, f32[2]{0:T(128)S(1)} %compare_convert_fusion), kind=kLoop, calls=%fused_computation.2 | loop fusion | flops 2048 | bytes 16392 | tf_op jit(solution)/shard_map/mul | solution.py:284
  1.6 0.2 copy.6
  1.8 3.5 %multiply_convert_fusion = bf16[1024,2,128]{2,1,0:T(2,128)(2,1)S(1)} fusion(bf16[1024,2,128]{2,1,0:T(2,128)(2,1)} %param.5, f32[1024,2]{1,0:T(8,128)S(1)} %copy.6), kind=kLoop, calls=%fused_computation | loop fusion | flops 786432 | bytes 1056768 | tf_op jit(solution)/shard_map/convert_element_type | solution.py:284
  5.3 0.1 copy.9
  5.4 0.0 copy-done
  5.4 0.0 copy-done.1
  5.4 80.1 %substitute.1 = bf16[2,128,1024]{2,1,0:T(8,128)(2,1)S(1)} custom-call(bf16[1024,1024]{1,0:T(8,128)(2,1)S(1)} %bitcast.7, bf16[1024,256]{1,0:T(8,128)(2,1)S(1)} %bitcast.9, bf16[2,128,1024]{2,1,0:T(8,128)(2,1)S(1)} %copy-done.1), custom_call_target="tpu_custom_call" | custom-call | tf_op jit(solution)/shard_map/substitute/pallas_call | solution.py:288
  85.5 2.5 %update.1 = bf16[1024,1024]{1,0:T(8,128)(2,1)} custom-call(bf16[1024,1024]{1,0:T(8,128)(2,1)S(1)} %bitcast.8, bf16[1024,256]{1,0:T(8,128)(2,1)S(1)} %bitcast.10, bf16[256,1024]{1,0:T(8,128)(2,1)S(1)} %bitcast.11), custom_call_target="tpu_custom_call" | custom-call | tf_op jit(solution)/shard_map/update/pallas_call | solution.py:310
  88.0 0.8 copy.11
  (1 shorter events, 0.0 us)
Async XLA Ops:
  0.6 4.7 %copy-start = (bf16[1024,1,1024]{2,0,1:T(8,128)(2,1)S(1)}, bf16[1024,1,1024]{2,0,1:T(8,128)(2,1)}, u32[]{:S(2)}) copy-start(bf16[1024,1,1024]{2,0,1:T(8,128)(2,1)} %param.4) | copy-start | bytes 6291460
  0.6 4.7 %copy-start.1 = (bf16[2,128,1024]{2,1,0:T(8,128)(2,1)S(1)}, bf16[2,128,1024]{2,1,0:T(8,128)(2,1)}, u32[]{:S(2)}) copy-start(bf16[2,128,1024]{2,1,0:T(8,128)(2,1)} %linv.1) | copy-start | bytes 1572868

commit v2 on v0

v2 whole, which is shorter than its diff:
```python
import functools

import jax
import jax.numpy as jnp
from jax import lax
from jax.experimental import pallas as pl
from jax.experimental.pallas import tpu as pltpu
from jax.sharding import PartitionSpec as P

MESH = pl.DeviceIdType.MESH
NX, NY, NZ = 4, 4, 16
BF = jnp.bfloat16
F32 = jnp.float32
FAR_FIRST = (8, 9, 7, 10, 6, 11, 5, 12, 4, 13, 3, 14, 2, 15, 1)


RELAYS = {0: (2, 6), 5: (4,), 2: (3,), 6: (7,)}
FIRST = (0, 1, 5)


def place(e):
    x = e // 2
    return x, (0 if e % 2 == 0 else (1 if x % 2 == 0 else NZ - 1)), x // 2


def comm_kernel(
    pend, panel, scale, linv, out, scaled,
    xin, part, fan, sol, prow, diff, linv_o, oblk,
    xs, xr, ps, pr, as_, ar, ls, lr, qs, qr, rs, zs, zr_, fs, fr,
):
    row, col = lax.axis_index("row"), lax.axis_index("col")
    x, z = row // NZ, row % NZ
    y, h = col // 2, col % 2
    other = 2 * y + (1 - h)
    second = jnp.where(x % 2 == 0, 1, NZ - 1)
    mine = h == x // 2
    lead_chip = jnp.logical_or(z == 0, z == second)
    lead = jnp.logical_and(lead_chip, mine)
    my_j = jnp.where(z == 0, 0, 1)
    my_e = jnp.where(lead, 2 * x + my_j, -1)
    source = [row == k for k in range(2)]
    my_rows = pl.ds(pl.multiple_of(y * 256, 256), 256)

    def dev(xx, zz, cc):
        return (xx * NZ + zz, cc)

    def solver(e, yy):
        ex, ez, eh = place(e)
        return dev(ex, ez, 2 * yy + eh)

    bar = pltpu.get_barrier_semaphore()

    def hello(target):
        pl.semaphore_signal(bar, inc=1, device_id=target, device_id_type=MESH)

    def both(p, q):
        return jnp.logical_and(p, q)

    def no(p):
        return jnp.logical_not(p)

    for yd in range(NY):
        sy = (y + yd) % NY
        if yd:
            @pl.when(lead)
            def _():
                hello((row, 2 * sy + h))
        for k in range(2):
            @pl.when(both(lead, no(source[k])) if yd == 0 else lead)
            def _():
                hello((k, 2 * sy + h))
        for e in FIRST:
            for hh in range(2):
                @pl.when(both(my_e == e, no(both(source[1], hh == h))) if yd == 0 else my_e == e)
                def _():
                    hello((1, 2 * sy + hh))
    for parent, children in RELAYS.items():
        for child in children:
            @pl.when(my_e == child)
            def _():
                hello(solver(parent, y))
    hello((row, other))
    lead_col = 2 * y + x // 2
    for lz in (0, second):
        @pl.when(z != lz)
        def _():
            hello(dev(x, lz, lead_col))
    for d in range(1, NX):
        hello(dev((x + d) % NX, z, col))
    expect = jnp.int32(1 + NX - 1) + jnp.where(lead, 2 * (NZ - 1) + NY - 1, 0)
    for k in range(2):
        expect += jnp.where(source[k], jnp.where(h == 0, 4 * NY - 1, 4 * NY), 0)
    expect += jnp.where(source[1], jnp.where(h == 0, 3 * NY - 1, 3 * NY), 0)
    for parent, children in RELAYS.items():
        expect += jnp.where(my_e == parent, len(children), 0)

    for k in range(2):
        active = jnp.where(row > k, 1.0, 0.0)

        def scale_rows(r, c):
            rows = pl.ds(pl.multiple_of(r * 256, 256), 256)
            s = jnp.broadcast_to(scale[k : k + 1, rows] * active, (128, 256)).T
            scaled[rows, k * 128 : (k + 1) * 128] = (panel[rows, k, :].astype(F32) * s).astype(BF)
            return c
        lax.fori_loop(0, 4, scale_rows, 0)

    pl.semaphore_wait(bar, expect)

    def remote(src, dst, send, recv, target):
        return pltpu.make_async_remote_copy(
            src, dst, send, recv, device_id=target, device_id_type=MESH)

    def linv_copy(k):
        return remote(linv.at[k], linv_o.at[k], ls.at[k], lr.at[k], (row, other))

    def lanes(i):
        return pl.ds(pl.multiple_of(i * 128, 128), 128)

    def swap_copy(i):
        return remote(pend.at[:, lanes(4 * (1 - h) + i)], xin.at[i], xs.at[i], xr.at[i], (row, other))

    def scatter_copy(k, i, yd):
        zz = 0 if i % 2 == 0 else (1 if i // 2 == 0 else NZ - 1)
        ty = (y + yd) % NY
        rows = pl.ds(pl.multiple_of(ty * 256, 256), 256)
        return remote(xin.at[i, rows], part.at[k, yd], ps.at[i, yd], pr.at[k, yd],
                      dev(2 * h + i // 2, zz, 2 * ty + h))

    def panel_copy(t, yd):
        ty = (y + yd) % NY
        rows = pl.ds(pl.multiple_of(ty * 256, 256), 256)
        return remote(scaled.at[rows, pl.ds(0, 128)], prow.at[:, lanes(col)], qs.at[t, yd], qr.at[col],
                      solver(FIRST[t], ty))

    def panel_wait(c):
        return remote(prow.at[:, lanes(c)], prow.at[:, lanes(c)], qs.at[0, 0], qr.at[c], (row, other))

    def relay_copy(child, n, c):
        return remote(prow.at[:, lanes(c)], prow.at[:, lanes(c)], rs.at[n, c], qr.at[c], solver(child, y))

    def gather_copy(buf, n, yd):
        return remote(buf.at[my_rows], buf.at[my_rows], as_.at[n, yd - 1], ar.at[n, yd - 1],
                      (row, 2 * ((y + yd) % NY) + h))

    def piece(k, xx, j):
        return out.at[k, :, lanes(2 * xx + j)]

    def line_copy(k, j, d, same):
        return remote(piece(k, x, j) if same else oblk.at[k], piece(k, x, j),
                      zs.at[k, d, 0 if same else 1], zr_.at[k, j],
                      dev(x, (z + d) % NZ, col if same else other))

    def spread_copy(k, j, d):
        return remote(piece(k, x, j), piece(k, x, j), fs.at[k, j, d - 1], fr.at[k, j, d - 1],
                      dev((x + d) % NX, z, col))

    def spread_wait(k, j, d):
        fx = (x + NX - d) % NX
        return remote(piece(k, fx, j), piece(k, fx, j), fs.at[k, j, d - 1], fr.at[k, j, d - 1],
                      dev(fx, z, col))

    def spread(k):
        for j in range(2):
            @pl.when(no(both(lead, my_j == j)))
            def _():
                line_copy(k, j, 0, False).wait_recv()
            for d in (2, 1, 3):
                spread_copy(k, j, d).start()

    def local_slot(k, i, yd):
        return i == k and yd == 0

    @pl.when(both(lead_chip, no(mine)))
    def _():
        for k in range(2):
            linv_copy(k).start()

    is_source = jnp.logical_or(source[0], source[1])

    @pl.when(is_source)
    def _():
        for i in range(4):
            swap_copy(i).start()

    @pl.when(source[1])
    def _():
        for t in range(3):
            for yd in range(NY):
                if t == 1 and yd == 0:
                    @pl.when(h == 0)
                    def _():
                        prow[:, lanes(col)] = scaled[my_rows, 0:128]

                    @pl.when(h != 0)
                    def _():
                        panel_copy(t, yd).start()
                else:
                    panel_copy(t, yd).start()

    @pl.when(is_source)
    def _():
        for i in range(4):
            swap_copy(i).wait_recv()

            def add(r, c):
                rows = pl.ds(pl.multiple_of(r * 256, 256), 256)
                xin[i, rows] = (pend[rows, lanes(4 * h + i)].astype(F32) + xin[i, rows].astype(F32)).astype(BF)
                return c
            lax.fori_loop(0, 4, add, 0)
            for k in range(2):
                @pl.when(source[k])
                def _():
                    for yd in range(NY):
                        if local_slot(k, i, yd):
                            @pl.when(h == 0)
                            def _():
                                part[k, 0] = xin[i, my_rows]

                            @pl.when(h != 0)
                            def _():
                                scatter_copy(k, i, yd).start()
                        else:
                            scatter_copy(k, i, yd).start()

    def reduced(k):
        @pl.when(no(source[k]))
        def _():
            scatter_copy(k, 0, 0).wait_recv()
        for yd in range(1, NY):
            scatter_copy(k, 0, yd).wait_recv()
        total = part[k, 0].astype(F32)
        for yd in range(1, NY):
            total += part[k, yd].astype(F32)
        return total

    def gather_start(buf, n):
        for yd in range(1, NY):
            gather_copy(buf, n, yd).start()

    def gather_wait(buf, n):
        for yd in range(1, NY):
            gather_copy(buf, n, yd).wait_recv()

    def solve(k):
        f = fan[k]
        block = jnp.dot(linv[k], f, preferred_element_type=F32).astype(BF)
        oblk[k] = jnp.dot(linv_o[k], f, preferred_element_type=F32).astype(BF)
        out[k, :, lanes(2 * x + my_j)] = block
        return block

    def line_start(k):
        for j in range(2):
            @pl.when(my_j == j)
            def _():
                for d in FAR_FIRST:
                    line_copy(k, j, d, False).start()
                    line_copy(k, j, d, True).start()
                line_copy(k, j, 0, False).start()

    @pl.when(lead)
    def _():
        fan[0, my_rows] = reduced(0).astype(BF)
        gather_start(fan.at[0], 0)
        for parent, children in RELAYS.items():
            @pl.when(my_e == parent)
            def _():
                for c in range(8):
                    panel_wait(c).wait_recv()
                    for n, child in enumerate(children):
                        relay_copy(child, n, c).start()
        for k in range(2):
            linv_copy(k).wait_recv()
        gather_wait(fan.at[0], 0)
        block = solve(0)
        sol[pl.ds(pl.multiple_of(col * 128, 128), 128)] = block
        sol[pl.ds(pl.multiple_of(other * 128, 128), 128)] = oblk[0]
        gather_start(sol, 1)
        line_start(0)
        diff[...] = reduced(1)
        relaying = jnp.bool_(False)
        for parent in RELAYS:
            relaying = jnp.logical_or(relaying, my_e == parent)
        for c in range(8):
            @pl.when(no(jnp.logical_or(relaying, both(source[1], c == col))))
            def _():
                panel_wait(c).wait_recv()
        gather_wait(sol, 1)
        fan[1, my_rows] = (
            diff[...] - jnp.dot(prow[...], sol[...], preferred_element_type=F32)).astype(BF)
        gather_start(fan.at[1], 2)
        spread(0)
        gather_wait(fan.at[1], 2)
        solve(1)
        line_start(1)

    @pl.when(no(lead))
    def _():
        spread(0)
    spread(1)

    for k in range(2):
        for j in range(2):
            for d in range(1, NX):
                spread_wait(k, j, d).wait_recv()

    for k in range(2):
        for j in range(2):
            for d in range(1, NX):
                spread_copy(k, j, d).wait_send()

    @pl.when(both(lead_chip, no(mine)))
    def _():
        for k in range(2):
            linv_copy(k).wait_send()

    for k in range(2):
        @pl.when(source[k])
        def _():
            for i in range(4):
                swap_copy(i).wait_send()
                for yd in range(NY):
                    if local_slot(k, i, yd):
                        @pl.when(h != 0)
                        def _():
                            scatter_copy(k, i, yd).wait_send()
                    else:
                        scatter_copy(k, i, yd).wait_send()

    @pl.when(source[1])
    def _():
        for t in range(3):
            for yd in range(NY):
                if t == 1 and yd == 0:
                    @pl.when(h != 0)
                    def _():
                        panel_copy(t, yd).wait_send()
                else:
                    panel_copy(t, yd).wait_send()

    @pl.when(lead)
    def _():
        for n, buf in enumerate((fan.at[0], sol, fan.at[1])):
            for yd in range(1, NY):
                gather_copy(buf, n, yd).wait_send()
        for k in range(2):
            for d in FAR_FIRST:
                line_copy(k, 0, d, False).wait_send()
                line_copy(k, 0, d, True).wait_send()
            line_copy(k, 0, 0, False).wait_send()
    for parent, children in RELAYS.items():
        @pl.when(my_e == parent)
        def _():
            for c in range(8):
                for n, child in enumerate(children):
                    relay_copy(child, n, c).wait_send()


def update_kernel(pend, scaled, solved, out):
    for c in range(4):
        cols = slice(c * 256, (c + 1) * 256)
        term = jnp.dot(scaled[...], solved[:, cols], preferred_element_type=F32)
        out[:, cols] = (pend[:, cols].astype(F32) - term).astype(BF)


def body(pending, panel, panel_scale, inverse_blocks):
    rows, _, cols = pending.shape
    current = pending.reshape(rows, cols)
    vmem = pl.BlockSpec(memory_space=pltpu.VMEM)
    dma = pltpu.SemaphoreType.DMA
    solved, scaled = pl.pallas_call(
        comm_kernel,
        out_shape=(jax.ShapeDtypeStruct((2, 128, cols), BF), jax.ShapeDtypeStruct((rows, 256), BF)),
        in_specs=[vmem] * 4,
        out_specs=(vmem, vmem),
        scratch_shapes=[
            pltpu.VMEM((4, rows, 128), BF),
            pltpu.VMEM((2, NY, 256, 128), BF),
            pltpu.VMEM((2, rows, 128), BF),
            pltpu.VMEM((rows, 128), BF),
            pltpu.VMEM((256, rows), BF),
            pltpu.VMEM((256, 128), F32),
            pltpu.VMEM((2, 128, cols), BF),
            pltpu.VMEM((2, 128, 128), BF),
            dma((4,)), dma((4,)), dma((4, NY)), dma((2, NY)),
            dma((3, NY - 1)), dma((3, NY - 1)), dma((2,)), dma((2,)),
            dma((3, NY)), dma((8,)), dma((2, 8)),
            dma((2, NZ, 2)), dma((2, 2)), dma((2, 2, NX - 1)), dma((2, 2, NX - 1)),
        ],
        compiler_params=pltpu.CompilerParams(
            collective_id=0, has_side_effects=True, vmem_limit_bytes=32 << 20),
        name="substitute",
    )(current, panel, panel_scale.T, inverse_blocks)
    tile = 256
    remaining = pl.pallas_call(
        update_kernel,
        grid=(rows // tile,),
        out_shape=jax.ShapeDtypeStruct((rows, cols), BF),
        in_specs=[
            pl.BlockSpec((tile, cols), lambda i: (i, 0)),
            pl.BlockSpec((tile, 256), lambda i: (i, 0)),
            pl.BlockSpec((256, cols), lambda i: (0, 0)),
        ],
        out_specs=pl.BlockSpec((tile, cols), lambda i: (i, 0)),
        compiler_params=pltpu.CompilerParams(vmem_limit_bytes=32 << 20),
        name="update",
    )(current, scaled, solved.reshape(256, cols))
    return remaining[:, None, :], solved


def solution(mesh):
    placed = (P("row", "col", None), P("row", None, "col"), P("row", None), P(None, "col", None))
    return jax.shard_map(
        body,
        mesh=mesh,
        in_specs=placed,
        out_specs=(P("row", "col", None), P(None, "col", None)),
        check_vma=False,
    )
```

time: 723 us -> 73 us (0.10)
  the two profiles are of different devices: /device:TPU:8 before, /device:TPU:32 now
where the time goes in v2:
time: 73 us; the launch traced here: 72.8 us
  Pallas kernels  66.9 us (92%)
  local copies, waits for them, and re-layouts  5.16 us (7%)
    pallas_call x1, Pallas kernels, body(): pl.pallas_call(comm_kernel, out_shape=(jax.ShapeDtypeStruct((2, 128, cols...  64.4 us
    unnamed x9, local copies, waits for them, and re-layouts  5.16 us
    pallas_call x1, Pallas kernels, body(): pl.pallas_call(update_kernel, grid=(rows // tile,), out_shape=jax.ShapeDt...  2.53 us

profile of v2, /device:TPU:32, one launch (start us, length us, event | category | flops | bytes accessed | tf_op | source)
XLA Modules:
  0.0 72.8 jit_solution(9687907907037415036)
XLA Ops:
  0.6 0.0 copy-start
  0.6 1.6 %copy-done = bf16[1024,1,1024]{2,0,1:T(8,128)(2,1)S(1)} copy-done((bf16[1024,1,1024]{2,0,1:T(8,128)(2,1)S(1)}, bf16[1024,1,1024]{2,0,1:T(8,128)(2,1)}, u32[]{:S(2)}) %copy-start) | copy-done | bytes 2097176
  2.2 0.0 copy-start.1
  2.2 1.0 %copy-done.1 = bf16[1024,2,128]{2,1,0:T(2,128)(2,1)S(1)} copy-done((bf16[1024,2,128]{2,1,0:T(2,128)(2,1)S(1)}, bf16[1024,2,128]{2,1,0:T(2,128)(2,1)}, u32[]{:S(2)}) %copy-start.1) | copy-done | bytes 524312
  3.3 0.0 copy-start.2
  3.3 1.0 %copy-done.2 = bf16[2,128,1024]{2,1,0:T(8,128)(2,1)S(1)} copy-done((bf16[2,128,1024]{2,1,0:T(8,128)(2,1)S(1)}, bf16[2,128,1024]{2,1,0:T(8,128)(2,1)}, u32[]{:S(2)}) %copy-start.2) | copy-done | bytes 524312
  4.3 0.0 copy-start.3
  4.3 0.7 copy-done.3
  5.0 64.4 %substitute.1 = (bf16[2,128,1024]{2,1,0:T(8,128)(2,1)S(1)}, bf16[1024,256]{1,0:T(8,128)(2,1)S(1)}) custom-call(bf16[1024,1024]{1,0:T(8,128)(2,1)S(1)} %bitcast.4, bf16[1024,2,128]{2,1,0:T(2,128)(2,1)S(1)} %copy-done.1, f32[2,1024]{1,0:T(2,128)S(1)} %bitcast.7, bf16[2,128,1024]{2,1,0:T(8,128)(2,1)S(1)} %copy-done.2), custom_call_target="tpu_custom_call" | custom-call | tf_op jit(solution)/shard_map/substitute/pallas_call | solution.py:370
  69.4 2.5 %update.1 = bf16[1024,1024]{1,0:T(8,128)(2,1)} custom-call(bf16[1024,1024]{1,0:T(8,128)(2,1)S(1)} %bitcast.5, bf16[1024,256]{1,0:T(8,128)(2,1)S(1)} %get-tuple-element.4.scaled, bf16[256,1024]{1,0:T(8,128)(2,1)S(1)} %bitcast.6), custom_call_target="tpu_custom_call" | custom-call | tf_op jit(solution)/shard_map/update/pallas_call | solution.py:394
  72.0 0.8 %copy.7 = bf16[2,128,1024]{2,1,0:T(8,128)(2,1)} copy(bf16[2,128,1024]{2,1,0:T(8,128)(2,1)S(1)} %get-tuple-element.9) | data formatting | bytes 1048576
Async XLA Ops:
  0.6 1.6 %copy-start = (bf16[1024,1,1024]{2,0,1:T(8,128)(2,1)S(1)}, bf16[1024,1,1024]{2,0,1:T(8,128)(2,1)}, u32[]{:S(2)}) copy-start(bf16[1024,1,1024]{2,0,1:T(8,128)(2,1)} %param.4) | copy-start | bytes 6291460
  2.2 1.0 %copy-start.1 = (bf16[1024,2,128]{2,1,0:T(2,128)(2,1)S(1)}, bf16[1024,2,128]{2,1,0:T(2,128)(2,1)}, u32[]{:S(2)}) copy-start(bf16[1024,2,128]{2,1,0:T(2,128)(2,1)} %panel.1) | copy-start | bytes 1572868
  3.3 1.0 %copy-start.2 = (bf16[2,128,1024]{2,1,0:T(8,128)(2,1)S(1)}, bf16[2,128,1024]{2,1,0:T(8,128)(2,1)}, u32[]{:S(2)}) copy-start(bf16[2,128,1024]{2,1,0:T(8,128)(2,1)} %linv.1) | copy-start | bytes 1572868
  4.3 0.7 copy-start.3

commit v3 on v2

--- a/solution.py
+++ b/solution.py
@@ -11,7 +11,8 @@
 NX, NY, NZ = 4, 4, 16
 BF = jnp.bfloat16
 F32 = jnp.float32
-FAR_FIRST = (8, 9, 7, 10, 6, 11, 5, 12, 4, 13, 3, 14, 2, 15, 1)
+DIRECT = (6, 10, 8, 4, 12, 3, 13, 2, 14, 1, 15)
+RELAYED = (5, 7, 9, 11)
 
 
 RELAYS = {0: (2, 6), 5: (4,), 2: (3,), 6: (7,)}
@@ -24,9 +25,9 @@
 
 
 def comm_kernel(
-    pend, panel, scale, linv, out, scaled,
-    xin, part, fan, sol, prow, diff, linv_o, oblk,
-    xs, xr, ps, pr, as_, ar, ls, lr, qs, qr, rs, zs, zr_, fs, fr,
+    pend, panel_in, scale_in, linv_in, out, scaled,
+    panel, scale, linv, pown, xin, part, fan, sol, prow, diff, linv_o, oblk,
+    ready, ld, lp, xs, xr, ps, pr, as_, ar, ls, lr, qs, qr, rs, zs, zr_, ts, fs, fr,
 ):
     row, col = lax.axis_index("row"), lax.axis_index("col")
     x, z = row // NZ, row % NZ
@@ -48,6 +49,30 @@
         ex, ez, eh = place(e)
         return dev(ex, ez, 2 * yy + eh)
 
+    is_source = jnp.logical_or(source[0], source[1])
+
+    def lanes(i):
+        return pl.ds(pl.multiple_of(i * 128, 128), 128)
+
+    def load(n):
+        src, dst = ((panel_in, panel), (scale_in, scale), (linv_in, linv))[n]
+        return pltpu.make_async_copy(src, dst, ld.at[n])
+
+    def load_own(i):
+        return pltpu.make_async_copy(pend.at[:, lanes(4 * h + i)], pown.at[i], lp.at[i])
+
+    load(0).start()
+    load(1).start()
+
+    @pl.when(lead)
+    def _():
+        load(2).start()
+
+    @pl.when(is_source)
+    def _():
+        for i in range(4):
+            load_own(i).start()
+
     bar = pltpu.get_barrier_semaphore()
 
     def hello(target):
@@ -81,40 +106,73 @@
                 hello(solver(parent, y))
     hello((row, other))
     lead_col = 2 * y + x // 2
-    for lz in (0, second):
-        @pl.when(z != lz)
+    line_z = (jnp.int32(0), second)
+    away = [(z - lz + NZ) % NZ for lz in line_z]
+
+    def among(v, values):
+        hit = v == values[0]
+        for w in values[1:]:
+            hit = jnp.logical_or(hit, v == w)
+        return hit
+
+    direct = [among(a, DIRECT) for a in away]
+    relayed = [among(a, RELAYED) for a in away]
+    relays = [among(a, (6, 10)) for a in away]
+    my_leads = jnp.where(direct[0], 1, 0) + jnp.where(direct[1], 1, 0)
+    for j in range(2):
+        @pl.when(relayed[j])
         def _():
-            hello(dev(x, lz, lead_col))
+            step = jnp.where(jnp.logical_or(away[j] == 7, away[j] == 11), NZ - 1, 1)
+            hello(dev(x, (z + step) % NZ, col))
+        my_leads += jnp.where(relays[j], 2, 0)
+
+    @pl.when(lead)
+    def _():
+        for d in DIRECT:
+            for hh in range(2):
+                hello(dev(x, (z + d) % NZ, 2 * y + hh))
     for d in range(1, NX):
         hello(dev((x + d) % NX, z, col))
-    expect = jnp.int32(1 + NX - 1) + jnp.where(lead, 2 * (NZ - 1) + NY - 1, 0)
+    expect = 1 + NX - 1 + my_leads + jnp.where(lead, NY - 1, 0)
     for k in range(2):
         expect += jnp.where(source[k], jnp.where(h == 0, 4 * NY - 1, 4 * NY), 0)
     expect += jnp.where(source[1], jnp.where(h == 0, 3 * NY - 1, 3 * NY), 0)
     for parent, children in RELAYS.items():
         expect += jnp.where(my_e == parent, len(children), 0)
 
-    for k in range(2):
-        active = jnp.where(row > k, 1.0, 0.0)
-
-        def scale_rows(r, c):
-            rows = pl.ds(pl.multiple_of(r * 256, 256), 256)
-            s = jnp.broadcast_to(scale[k : k + 1, rows] * active, (128, 256)).T
-            scaled[rows, k * 128 : (k + 1) * 128] = (panel[rows, k, :].astype(F32) * s).astype(BF)
-            return c
-        lax.fori_loop(0, 4, scale_rows, 0)
+    def scale_panel():
+        load(0).wait()
+        load(1).wait()
+        for k in range(2):
+            active = jnp.where(row > k, 1.0, 0.0)
+
+            def scale_rows(r, c):
+                rows = pl.ds(pl.multiple_of(r * 256, 256), 256)
+                s = jnp.broadcast_to(scale[k : k + 1, rows] * active, (128, 256)).T
+                scaled[rows, k * 128 : (k + 1) * 128] = (panel[rows, k, :].astype(F32) * s).astype(BF)
+                return c
+            lax.fori_loop(0, 4, scale_rows, 0)
+
+    early = jnp.logical_or(source[1], no(jnp.logical_or(source[0], lead)))
+
+    @pl.when(early)
+    def _():
+        scale_panel()
 
     pl.semaphore_wait(bar, expect)
+
+    for j in range(2):
+        @pl.when(direct[j])
+        def _():
+            pl.semaphore_signal(
+                ready, inc=1, device_id=dev(x, line_z[j], lead_col), device_id_type=MESH)
 
     def remote(src, dst, send, recv, target):
         return pltpu.make_async_remote_copy(
             src, dst, send, recv, device_id=target, device_id_type=MESH)
 
     def linv_copy(k):
-        return remote(linv.at[k], linv_o.at[k], ls.at[k], lr.at[k], (row, other))
-
-    def lanes(i):
-        return pl.ds(pl.multiple_of(i * 128, 128), 128)
+        return remote(linv_in.at[k], linv_o.at[k], ls.at[k], lr.at[k], (row, other))
 
     def swap_copy(i):
         return remote(pend.at[:, lanes(4 * (1 - h) + i)], xin.at[i], xs.at[i], xr.at[i], (row, other))
@@ -150,6 +208,10 @@
                       zs.at[k, d, 0 if same else 1], zr_.at[k, j],
                       dev(x, (z + d) % NZ, col if same else other))
 
+    def pass_copy(k, j, n):
+        return remote(piece(k, x, j), piece(k, x, j), ts.at[k, n], zr_.at[k, j],
+                      dev(x, (z + (1, NZ - 1)[n]) % NZ, col))
+
     def spread_copy(k, j, d):
         return remote(piece(k, x, j), piece(k, x, j), fs.at[k, j, d - 1], fr.at[k, j, d - 1],
                       dev((x + d) % NX, z, col))
@@ -164,6 +226,11 @@
             @pl.when(no(both(lead, my_j == j)))
             def _():
                 line_copy(k, j, 0, False).wait_recv()
+
+            @pl.when(relays[j])
+            def _():
+                for n in range(2):
+                    pass_copy(k, j, n).start()
             for d in (2, 1, 3):
                 spread_copy(k, j, d).start()
 
@@ -174,8 +241,6 @@
     def _():
         for k in range(2):
             linv_copy(k).start()
-
-    is_source = jnp.logical_or(source[0], source[1])
 
     @pl.when(is_source)
     def _():
@@ -200,11 +265,12 @@
     @pl.when(is_source)
     def _():
         for i in range(4):
+            load_own(i).wait()
             swap_copy(i).wait_recv()
 
             def add(r, c):
                 rows = pl.ds(pl.multiple_of(r * 256, 256), 256)
-                xin[i, rows] = (pend[rows, lanes(4 * h + i)].astype(F32) + xin[i, rows].astype(F32)).astype(BF)
+                xin[i, rows] = (pown[i, rows].astype(F32) + xin[i, rows].astype(F32)).astype(BF)
                 return c
             lax.fori_loop(0, 4, add, 0)
             for k in range(2):
@@ -234,7 +300,7 @@
         return total
 
     def gather_start(buf, n):
-        for yd in range(1, NY):
+        for yd in (2, 1, 3):
             gather_copy(buf, n, yd).start()
 
     def gather_wait(buf, n):
@@ -252,7 +318,7 @@
         for j in range(2):
             @pl.when(my_j == j)
             def _():
-                for d in FAR_FIRST:
+                for d in DIRECT:
                     line_copy(k, j, d, False).start()
                     line_copy(k, j, d, True).start()
                 line_copy(k, j, 0, False).start()
@@ -270,11 +336,13 @@
                         relay_copy(child, n, c).start()
         for k in range(2):
             linv_copy(k).wait_recv()
+        load(2).wait()
         gather_wait(fan.at[0], 0)
         block = solve(0)
         sol[pl.ds(pl.multiple_of(col * 128, 128), 128)] = block
         sol[pl.ds(pl.multiple_of(other * 128, 128), 128)] = oblk[0]
         gather_start(sol, 1)
+        pl.semaphore_wait(ready, 2 * len(DIRECT))
         line_start(0)
         diff[...] = reduced(1)
         relaying = jnp.bool_(False)
@@ -296,6 +364,10 @@
     @pl.when(no(lead))
     def _():
         spread(0)
+
+    @pl.when(no(early))
+    def _():
+        scale_panel()
     spread(1)
 
     for k in range(2):
@@ -307,6 +379,11 @@
         for j in range(2):
             for d in range(1, NX):
                 spread_copy(k, j, d).wait_send()
+
+            @pl.when(relays[j])
+            def _():
+                for n in range(2):
+                    pass_copy(k, j, n).wait_send()
 
     @pl.when(both(lead_chip, no(mine)))
     def _():
@@ -343,7 +420,7 @@
             for yd in range(1, NY):
                 gather_copy(buf, n, yd).wait_send()
         for k in range(2):
-            for d in FAR_FIRST:
+            for d in DIRECT:
                 line_copy(k, 0, d, False).wait_send()
                 line_copy(k, 0, d, True).wait_send()
             line_copy(k, 0, 0, False).wait_send()
@@ -355,24 +432,46 @@
                     relay_copy(child, n, c).wait_send()
 
 
-def update_kernel(pend, scaled, solved, out):
-    for c in range(4):
-        cols = slice(c * 256, (c + 1) * 256)
-        term = jnp.dot(scaled[...], solved[:, cols], preferred_element_type=F32)
-        out[:, cols] = (pend[:, cols].astype(F32) - term).astype(BF)
+def update_kernel(pend, scaled, solved, out, solved_out, done, sem):
+    tiles = done.shape[0]
+    size = done.shape[1]
+    last = pltpu.make_async_copy(solved, solved_out, sem.at[tiles])
+    last.start()
+
+    def store(i):
+        return pltpu.make_async_copy(
+            done.at[i], out.at[pl.ds(pl.multiple_of(i * size, size), size)], sem.at[i])
+
+    def tile(i, c):
+        rows = pl.ds(pl.multiple_of(i * size, size), size)
+        for n in range(4):
+            cols = slice(n * 256, (n + 1) * 256)
+            term = jnp.dot(scaled[rows], solved[:, cols], preferred_element_type=F32)
+            done[i, :, cols] = (pend[rows, cols].astype(F32) - term).astype(BF)
+        store(i).start()
+        return c
+    lax.fori_loop(0, tiles, tile, 0)
+    for i in range(tiles):
+        store(i).wait()
+    last.wait()
 
 
 def body(pending, panel, panel_scale, inverse_blocks):
     rows, _, cols = pending.shape
     current = pending.reshape(rows, cols)
     vmem = pl.BlockSpec(memory_space=pltpu.VMEM)
+    hbm = pl.BlockSpec(memory_space=pltpu.HBM)
     dma = pltpu.SemaphoreType.DMA
     solved, scaled = pl.pallas_call(
         comm_kernel,
         out_shape=(jax.ShapeDtypeStruct((2, 128, cols), BF), jax.ShapeDtypeStruct((rows, 256), BF)),
-        in_specs=[vmem] * 4,
+        in_specs=[hbm] * 4,
         out_specs=(vmem, vmem),
         scratch_shapes=[
+            pltpu.VMEM((rows, 2, 128), BF),
+            pltpu.VMEM((2, rows), F32),
+            pltpu.VMEM((2, 128, rows), BF),
+            pltpu.VMEM((4, rows, 128), BF),
             pltpu.VMEM((4, rows, 128), BF),
             pltpu.VMEM((2, NY, 256, 128), BF),
             pltpu.VMEM((2, rows, 128), BF),
@@ -381,30 +480,27 @@
             pltpu.VMEM((256, 128), F32),
             pltpu.VMEM((2, 128, cols), BF),
             pltpu.VMEM((2, 128, 128), BF),
+            pltpu.SemaphoreType.REGULAR, dma((3,)), dma((4,)),
             dma((4,)), dma((4,)), dma((4, NY)), dma((2, NY)),
             dma((3, NY - 1)), dma((3, NY - 1)), dma((2,)), dma((2,)),
             dma((3, NY)), dma((8,)), dma((2, 8)),
-            dma((2, NZ, 2)), dma((2, 2)), dma((2, 2, NX - 1)), dma((2, 2, NX - 1)),
+            dma((2, NZ, 2)), dma((2, 2)), dma((2, 2)), dma((2, 2, NX - 1)), dma((2, 2, NX - 1)),
         ],
         compiler_params=pltpu.CompilerParams(
             collective_id=0, has_side_effects=True, vmem_limit_bytes=32 << 20),
         name="substitute",
-    )(current, panel, panel_scale.T, inverse_blocks)
-    tile = 256
-    remaining = pl.pallas_call(
+    )(*(pltpu.with_memory_space_constraint(v, pltpu.HBM)
+        for v in (current, panel, panel_scale.T, inverse_blocks)))
+    remaining, solved = pl.pallas_call(
         update_kernel,
-        grid=(rows // tile,),
-        out_shape=jax.ShapeDtypeStruct((rows, cols), BF),
-        in_specs=[
-            pl.BlockSpec((tile, cols), lambda i: (i, 0)),
-            pl.BlockSpec((tile, 256), lambda i: (i, 0)),
-            pl.BlockSpec((256, cols), lambda i: (0, 0)),
-        ],
-        out_specs=pl.BlockSpec((tile, cols), lambda i: (i, 0)),
+        out_shape=(jax.ShapeDtypeStruct((rows, cols), BF), jax.ShapeDtypeStruct((256, cols), BF)),
+        in_specs=[vmem] * 3,
+        out_specs=(hbm, hbm),
+        scratch_shapes=[pltpu.VMEM((8, rows // 8, cols), BF), dma((9,))],
         compiler_params=pltpu.CompilerParams(vmem_limit_bytes=32 << 20),
         name="update",
     )(current, scaled, solved.reshape(256, cols))
-    return remaining[:, None, :], solved
+    return remaining[:, None, :], solved.reshape(2, 128, cols)
 
 
 def solution(mesh):

time: 73 us -> 64.9 us (0.89)
  local copies, waits for them, and re-layouts: 5.16 us -> 0.01 us
  Pallas kernels: 66.9 us -> 64.2 us
    unnamed x9 -> x2, local copies, waits for them, and re-layouts: 5.16 us -> 0.01 us
    pallas_call x1, Pallas kernels: 64.4 us -> 61.5 us  [body(): pl.pallas_call(comm_kernel, out_shape=(jax.ShapeDtypeStruct((2, 128, cols...]
where the time goes in v3:
time: 64.9 us; the launch traced here: 64.8 us
  Pallas kernels  64.2 us (99%)
  between operations  0.65 us (1%)
    pallas_call x1, Pallas kernels, body(): pl.pallas_call(comm_kernel, out_shape=(jax.ShapeDtypeStruct((2, 128, cols...  61.5 us
    pallas_call x1, Pallas kernels, body(): pl.pallas_call(update_kernel, out_shape=(jax.ShapeDtypeStruct((rows, cols...  2.69 us

profile of v3, /device:TPU:32, one launch (start us, length us, event | category | flops | bytes accessed | tf_op | source)
XLA Modules:
  0.0 64.8 jit_solution(1480764624934086217)
XLA Ops:
  0.6 0.0 copy-start
  0.6 61.5 %substitute.1 = (bf16[2,128,1024]{2,1,0:T(8,128)(2,1)S(1)}, bf16[1024,256]{1,0:T(8,128)(2,1)S(1)}) custom-call(bf16[1024,1024]{1,0:T(8,128)(2,1)} %bitcast.5, bf16[1024,2,128]{2,1,0:T(2,128)(2,1)} %panel_in.1, f32[2,1024]{1,0:T(2,128)} %bitcast.8, bf16[2,128,1024]{2,1,0:T(8,128)(2,1)} %linv_in.1), custom_call_target="tpu_custom_call" | custom-call | tf_op jit(solution)/shard_map/substitute/pallas_call | solution.py:465
  62.1 0.0 copy-done
  62.1 2.7 %update.1 = (bf16[1024,1024]{1,0:T(8,128)(2,1)}, bf16[256,1024]{1,0:T(8,128)(2,1)}) custom-call(bf16[1024,1024]{1,0:T(8,128)(2,1)S(1)} %bitcast.6, bf16[1024,256]{1,0:T(8,128)(2,1)S(1)} %get-tuple-element.6.scaled, bf16[256,1024]{1,0:T(8,128)(2,1)S(1)} %bitcast.7), custom_call_target="tpu_custom_call" | custom-call | tf_op jit(solution)/shard_map/update/pallas_call | solution.py:494
Async XLA Ops:
  0.6 61.5 %copy-start = (bf16[1024,1,1024]{2,0,1:T(8,128)(2,1)S(1)}, bf16[1024,1,1024]{2,0,1:T(8,128)(2,1)}, u32[]{:S(2)}) copy-start(bf16[1024,1,1024]{2,0,1:T(8,128)(2,1)} %param.4) | copy-start | bytes 6291460

commit v4 on v3

--- a/solution.py
+++ b/solution.py
@@ -15,8 +15,11 @@
 RELAYED = (5, 7, 9, 11)
 
 
-RELAYS = {0: (2, 6), 5: (4,), 2: (3,), 6: (7,)}
-FIRST = (0, 1, 5)
+CHILDREN = {8: (6, 5, 1), 6: (7, 0, 4), 5: (2,), 1: (3,)}
+ADDERS = ((1, 1), (0, 2), (0, 3), (3, 1))
+
+
+ORDER = ((1, 2, 3, 0), (1, 2, 3, 0))
 
 
 def place(e):
@@ -24,10 +27,17 @@
     return x, (0 if e % 2 == 0 else (1 if x % 2 == 0 else NZ - 1)), x // 2
 
 
+def node_place(n):
+    if n == 8:
+        return 3, 1, 0
+    x, z, core = place(n)
+    return x, z, 1 - core
+
+
 def comm_kernel(
     pend, panel_in, scale_in, linv_in, out, scaled,
-    panel, scale, linv, pown, xin, part, fan, sol, prow, diff, linv_o, oblk,
-    ready, ld, lp, xs, xr, ps, pr, as_, ar, ls, lr, qs, qr, rs, zs, zr_, ts, fs, fr,
+    panel, scale, linv, pown, xin, part, fan, sol, prow, acc, diff, oblk,
+    ready, ld, lp, xs, xr, ps, pr, as_, ar, ls, lr, qs, qr, rs, us, ds_, dr, zs, zr_, ts, fs, fr,
 ):
     row, col = lax.axis_index("row"), lax.axis_index("col")
     x, z = row // NZ, row % NZ
@@ -40,6 +50,12 @@
     my_j = jnp.where(z == 0, 0, 1)
     my_e = jnp.where(lead, 2 * x + my_j, -1)
     source = [row == k for k in range(2)]
+    my_node = jnp.where(jnp.logical_and(lead_chip, jnp.logical_not(mine)), 2 * x + my_j, -1)
+    my_node = jnp.where(jnp.logical_and(row == 3 * NZ + 1, h == 0), 8, my_node)
+    my_add = jnp.int32(-1)
+    for i, (ax, az) in enumerate(ADDERS):
+        my_add = jnp.where(row == ax * NZ + az, i, my_add)
+    adder = my_add >= 0
     my_rows = pl.ds(pl.multiple_of(y * 256, 256), 256)
 
     def dev(xx, zz, cc):
@@ -51,11 +67,15 @@
 
     is_source = jnp.logical_or(source[0], source[1])
 
+    def node(n, yy):
+        nx, nz, nh = node_place(n)
+        return dev(nx, nz, 2 * yy + nh)
+
     def lanes(i):
         return pl.ds(pl.multiple_of(i * 128, 128), 128)
 
     def load(n):
-        src, dst = ((panel_in, panel), (scale_in, scale), (linv_in, linv))[n]
+        src, dst = ((panel_in, panel), (scale_in, scale), (linv_in, linv.at[:, pl.ds(0, 128)]))[n]
         return pltpu.make_async_copy(src, dst, ld.at[n])
 
     def load_own(i):
@@ -90,20 +110,27 @@
             @pl.when(lead)
             def _():
                 hello((row, 2 * sy + h))
-        for k in range(2):
-            @pl.when(both(lead, no(source[k])) if yd == 0 else lead)
-            def _():
-                hello((k, 2 * sy + h))
-        for e in FIRST:
+        @pl.when(both(lead, no(source[0])) if yd == 0 else lead)
+        def _():
+            hello((0, 2 * sy + h))
+
+        @pl.when(adder)
+        def _():
+            hello((1, 2 * sy + h))
+
+        @pl.when(my_node == 8)
+        def _():
             for hh in range(2):
-                @pl.when(both(my_e == e, no(both(source[1], hh == h))) if yd == 0 else my_e == e)
-                def _():
-                    hello((1, 2 * sy + hh))
-    for parent, children in RELAYS.items():
+                hello((1, 2 * sy + hh))
+    for parent, children in CHILDREN.items():
         for child in children:
-            @pl.when(my_e == child)
-            def _():
-                hello(solver(parent, y))
+            @pl.when(my_node == child)
+            def _():
+                hello(node(parent, y))
+    for i, (ax, az) in enumerate(ADDERS):
+        @pl.when(both(lead, my_e % 4 == i))
+        def _():
+            hello(dev(ax, az, col))
     hello((row, other))
     lead_col = 2 * y + x // 2
     line_z = (jnp.int32(0), second)
@@ -134,11 +161,11 @@
     for d in range(1, NX):
         hello(dev((x + d) % NX, z, col))
     expect = 1 + NX - 1 + my_leads + jnp.where(lead, NY - 1, 0)
-    for k in range(2):
-        expect += jnp.where(source[k], jnp.where(h == 0, 4 * NY - 1, 4 * NY), 0)
-    expect += jnp.where(source[1], jnp.where(h == 0, 3 * NY - 1, 3 * NY), 0)
-    for parent, children in RELAYS.items():
-        expect += jnp.where(my_e == parent, len(children), 0)
+    expect += jnp.where(source[0], jnp.where(h == 0, 4 * NY - 1, 4 * NY), 0)
+    expect += jnp.where(source[1], 4 * NY + NY, 0)
+    expect += jnp.where(adder, 1, 0)
+    for parent, children in CHILDREN.items():
+        expect += jnp.where(my_node == parent, len(children), 0)
 
     def scale_panel():
         load(0).wait()
@@ -172,29 +199,39 @@
             src, dst, send, recv, device_id=target, device_id_type=MESH)
 
     def linv_copy(k):
-        return remote(linv_in.at[k], linv_o.at[k], ls.at[k], lr.at[k], (row, other))
+        return remote(linv_in.at[k], linv.at[k, pl.ds(128, 128)], ls.at[k], lr.at[k], (row, other))
 
     def swap_copy(i):
         return remote(pend.at[:, lanes(4 * (1 - h) + i)], xin.at[i], xs.at[i], xr.at[i], (row, other))
 
     def scatter_copy(k, i, yd):
         zz = 0 if i % 2 == 0 else (1 if i // 2 == 0 else NZ - 1)
+        tx = 2 * h + i // 2
+        if k == 1:
+            tx, zz = ADDERS[i]
         ty = (y + yd) % NY
         rows = pl.ds(pl.multiple_of(ty * 256, 256), 256)
         return remote(xin.at[i, rows], part.at[k, yd], ps.at[i, yd], pr.at[k, yd],
-                      dev(2 * h + i // 2, zz, 2 * ty + h))
-
-    def panel_copy(t, yd):
+                      dev(tx, zz, 2 * ty + h))
+
+    def panel_copy(yd):
         ty = (y + yd) % NY
         rows = pl.ds(pl.multiple_of(ty * 256, 256), 256)
-        return remote(scaled.at[rows, pl.ds(0, 128)], prow.at[:, lanes(col)], qs.at[t, yd], qr.at[col],
-                      solver(FIRST[t], ty))
+        return remote(scaled.at[rows, pl.ds(0, 128)], prow.at[:, lanes(col)], qs.at[yd], qr.at[col],
+                      node(8, ty))
 
     def panel_wait(c):
-        return remote(prow.at[:, lanes(c)], prow.at[:, lanes(c)], qs.at[0, 0], qr.at[c], (row, other))
+        return remote(prow.at[:, lanes(c)], prow.at[:, lanes(c)], qs.at[0], qr.at[c], (row, other))
 
     def relay_copy(child, n, c):
-        return remote(prow.at[:, lanes(c)], prow.at[:, lanes(c)], rs.at[n, c], qr.at[c], solver(child, y))
+        return remote(prow.at[:, lanes(c)], prow.at[:, lanes(c)], rs.at[n, c], qr.at[c], node(child, y))
+
+    def mate_copy(c):
+        return remote(prow.at[:, lanes(c)], prow.at[:, lanes(c)], us.at[c], qr.at[c], (row, other))
+
+    def diff_copy(i):
+        tz = 0 if i % 2 == 0 else (1 if i // 2 == 0 else NZ - 1)
+        return remote(acc, diff, ds_, dr, dev(2 * h + i // 2, tz, col))
 
     def gather_copy(buf, n, yd):
         return remote(buf.at[my_rows], buf.at[my_rows], as_.at[n, yd - 1], ar.at[n, yd - 1],
@@ -234,8 +271,13 @@
             for d in (2, 1, 3):
                 spread_copy(k, j, d).start()
 
-    def local_slot(k, i, yd):
-        return i == k and yd == 0
+    def unless_local(k, i, yd, action, local=None):
+        if not (k == 0 and i == 0 and yd == 0):
+            action()
+        else:
+            pl.when(h != 0)(action)
+            if local:
+                pl.when(h == 0)(local)
 
     @pl.when(both(lead_chip, no(mine)))
     def _():
@@ -244,54 +286,42 @@
 
     @pl.when(is_source)
     def _():
-        for i in range(4):
-            swap_copy(i).start()
+        for k in range(2):
+            @pl.when(source[k])
+            def _():
+                for i in ORDER[k]:
+                    swap_copy(i).start()
 
     @pl.when(source[1])
     def _():
-        for t in range(3):
-            for yd in range(NY):
-                if t == 1 and yd == 0:
-                    @pl.when(h == 0)
-                    def _():
-                        prow[:, lanes(col)] = scaled[my_rows, 0:128]
-
-                    @pl.when(h != 0)
-                    def _():
-                        panel_copy(t, yd).start()
-                else:
-                    panel_copy(t, yd).start()
-
-    @pl.when(is_source)
-    def _():
-        for i in range(4):
-            load_own(i).wait()
-            swap_copy(i).wait_recv()
-
-            def add(r, c):
-                rows = pl.ds(pl.multiple_of(r * 256, 256), 256)
-                xin[i, rows] = (pown[i, rows].astype(F32) + xin[i, rows].astype(F32)).astype(BF)
-                return c
-            lax.fori_loop(0, 4, add, 0)
-            for k in range(2):
-                @pl.when(source[k])
-                def _():
-                    for yd in range(NY):
-                        if local_slot(k, i, yd):
-                            @pl.when(h == 0)
-                            def _():
-                                part[k, 0] = xin[i, my_rows]
-
-                            @pl.when(h != 0)
-                            def _():
-                                scatter_copy(k, i, yd).start()
-                        else:
-                            scatter_copy(k, i, yd).start()
+        for yd in range(NY):
+            panel_copy(yd).start()
+
+    for k in range(2):
+        @pl.when(source[k])
+        def _():
+            for i in ORDER[k]:
+                load_own(i).wait()
+                swap_copy(i).wait_recv()
+
+                def add(r, c):
+                    rows = pl.ds(pl.multiple_of(r * 256, 256), 256)
+                    xin[i, rows] = (pown[i, rows].astype(F32) + xin[i, rows].astype(F32)).astype(BF)
+                    return c
+                lax.fori_loop(0, 4, add, 0)
+
+                def keep():
+                    part[k, 0] = xin[i, my_rows]
+                for yd in (2, 1, 3, 0):
+                    unless_local(k, i, yd, lambda: scatter_copy(k, i, yd).start(), keep)
 
     def reduced(k):
-        @pl.when(no(source[k]))
-        def _():
+        if k == 1:
             scatter_copy(k, 0, 0).wait_recv()
+        else:
+            @pl.when(no(source[0]))
+            def _():
+                scatter_copy(k, 0, 0).wait_recv()
         for yd in range(1, NY):
             scatter_copy(k, 0, yd).wait_recv()
         total = part[k, 0].astype(F32)
@@ -308,11 +338,10 @@
             gather_copy(buf, n, yd).wait_recv()
 
     def solve(k):
-        f = fan[k]
-        block = jnp.dot(linv[k], f, preferred_element_type=F32).astype(BF)
-        oblk[k] = jnp.dot(linv_o[k], f, preferred_element_type=F32).astype(BF)
-        out[k, :, lanes(2 * x + my_j)] = block
-        return block
+        blocks = jnp.dot(linv[k], fan[k], preferred_element_type=F32).astype(BF)
+        oblk[k] = blocks[128:]
+        out[k, :, lanes(2 * x + my_j)] = blocks[:128]
+        return blocks
 
     def line_start(k):
         for j in range(2):
@@ -323,35 +352,46 @@
                     line_copy(k, j, d, True).start()
                 line_copy(k, j, 0, False).start()
 
+    def add_up():
+        @pl.when(adder)
+        def _():
+            acc[...] = reduced(1)
+            for i in range(4):
+                @pl.when(my_add == i)
+                def _():
+                    diff_copy(i).start()
+
+    @pl.when(my_node >= 0)
+    def _():
+        for c in range(8):
+            panel_wait(c).wait_recv()
+            for parent, children in CHILDREN.items():
+                @pl.when(my_node == parent)
+                def _():
+                    for n, child in enumerate(children):
+                        relay_copy(child, n, c).start()
+
+            @pl.when(my_node != 8)
+            def _():
+                mate_copy(c).start()
+
     @pl.when(lead)
     def _():
         fan[0, my_rows] = reduced(0).astype(BF)
         gather_start(fan.at[0], 0)
-        for parent, children in RELAYS.items():
-            @pl.when(my_e == parent)
-            def _():
-                for c in range(8):
-                    panel_wait(c).wait_recv()
-                    for n, child in enumerate(children):
-                        relay_copy(child, n, c).start()
         for k in range(2):
             linv_copy(k).wait_recv()
         load(2).wait()
         gather_wait(fan.at[0], 0)
-        block = solve(0)
-        sol[pl.ds(pl.multiple_of(col * 128, 128), 128)] = block
-        sol[pl.ds(pl.multiple_of(other * 128, 128), 128)] = oblk[0]
+        blocks = solve(0)
+        sol[pl.ds(pl.multiple_of(col * 128, 128), 128)] = blocks[:128]
+        sol[pl.ds(pl.multiple_of(other * 128, 128), 128)] = blocks[128:]
         gather_start(sol, 1)
         pl.semaphore_wait(ready, 2 * len(DIRECT))
         line_start(0)
-        diff[...] = reduced(1)
-        relaying = jnp.bool_(False)
-        for parent in RELAYS:
-            relaying = jnp.logical_or(relaying, my_e == parent)
+        diff_copy(0).wait_recv()
         for c in range(8):
-            @pl.when(no(jnp.logical_or(relaying, both(source[1], c == col))))
-            def _():
-                panel_wait(c).wait_recv()
+            panel_wait(c).wait_recv()
         gather_wait(sol, 1)
         fan[1, my_rows] = (
             diff[...] - jnp.dot(prow[...], sol[...], preferred_element_type=F32)).astype(BF)
@@ -363,6 +403,7 @@
 
     @pl.when(no(lead))
     def _():
+        add_up()
         spread(0)
 
     @pl.when(no(early))
@@ -396,23 +437,12 @@
             for i in range(4):
                 swap_copy(i).wait_send()
                 for yd in range(NY):
-                    if local_slot(k, i, yd):
-                        @pl.when(h != 0)
-                        def _():
-                            scatter_copy(k, i, yd).wait_send()
-                    else:
-                        scatter_copy(k, i, yd).wait_send()
+                    unless_local(k, i, yd, lambda: scatter_copy(k, i, yd).wait_send())
 
     @pl.when(source[1])
     def _():
-        for t in range(3):
-            for yd in range(NY):
-                if t == 1 and yd == 0:
-                    @pl.when(h != 0)
-                    def _():
-                        panel_copy(t, yd).wait_send()
-                else:
-                    panel_copy(t, yd).wait_send()
+        for yd in range(NY):
+            panel_copy(yd).wait_send()
 
     @pl.when(lead)
     def _():
@@ -424,30 +454,38 @@
                 line_copy(k, 0, d, False).wait_send()
                 line_copy(k, 0, d, True).wait_send()
             line_copy(k, 0, 0, False).wait_send()
-    for parent, children in RELAYS.items():
-        @pl.when(my_e == parent)
-        def _():
-            for c in range(8):
-                for n, child in enumerate(children):
-                    relay_copy(child, n, c).wait_send()
+    @pl.when(adder)
+    def _():
+        diff_copy(0).wait_send()
+
+    @pl.when(my_node >= 0)
+    def _():
+        for c in range(8):
+            for parent, children in CHILDREN.items():
+                @pl.when(my_node == parent)
+                def _():
+                    for n, child in enumerate(children):
+                        relay_copy(child, n, c).wait_send()
+
+            @pl.when(my_node != 8)
+            def _():
+                mate_copy(c).wait_send()
 
 
 def update_kernel(pend, scaled, solved, out, solved_out, done, sem):
     tiles = done.shape[0]
-    size = done.shape[1]
+    size = done.shape[2]
     last = pltpu.make_async_copy(solved, solved_out, sem.at[tiles])
     last.start()
 
     def store(i):
         return pltpu.make_async_copy(
-            done.at[i], out.at[pl.ds(pl.multiple_of(i * size, size), size)], sem.at[i])
+            done.at[i], out.at[:, pl.ds(pl.multiple_of(i * size, size), size)], sem.at[i])
 
     def tile(i, c):
-        rows = pl.ds(pl.multiple_of(i * size, size), size)
-        for n in range(4):
-            cols = slice(n * 256, (n + 1) * 256)
-            term = jnp.dot(scaled[rows], solved[:, cols], preferred_element_type=F32)
-            done[i, :, cols] = (pend[rows, cols].astype(F32) - term).astype(BF)
+        cols = pl.ds(pl.multiple_of(i * size, size), size)
+        term = jnp.dot(scaled[...], solved[:, cols], preferred_element_type=F32)
+        done[i] = (pend[:, cols].astype(F32) - term).astype(BF)
         store(i).start()
         return c
     lax.fori_loop(0, tiles, tile, 0)
@@ -470,7 +508,7 @@
         scratch_shapes=[
             pltpu.VMEM((rows, 2, 128), BF),
             pltpu.VMEM((2, rows), F32),
-            pltpu.VMEM((2, 128, rows), BF),
+            pltpu.VMEM((2, 256, rows), BF),
             pltpu.VMEM((4, rows, 128), BF),
             pltpu.VMEM((4, rows, 128), BF),
             pltpu.VMEM((2, NY, 256, 128), BF),
@@ -478,12 +516,12 @@
             pltpu.VMEM((rows, 128), BF),
             pltpu.VMEM((256, rows), BF),
             pltpu.VMEM((256, 128), F32),
-            pltpu.VMEM((2, 128, cols), BF),
+            pltpu.VMEM((256, 128), F32),
             pltpu.VMEM((2, 128, 128), BF),
             pltpu.SemaphoreType.REGULAR, dma((3,)), dma((4,)),
             dma((4,)), dma((4,)), dma((4, NY)), dma((2, NY)),
             dma((3, NY - 1)), dma((3, NY - 1)), dma((2,)), dma((2,)),
-            dma((3, NY)), dma((8,)), dma((2, 8)),
+            dma((NY,)), dma((8,)), dma((3, 8)), dma((8,)), dma, dma,
             dma((2, NZ, 2)), dma((2, 2)), dma((2, 2)), dma((2, 2, NX - 1)), dma((2, 2, NX - 1)),
         ],
         compiler_params=pltpu.CompilerParams(
@@ -496,7 +534,7 @@
         out_shape=(jax.ShapeDtypeStruct((rows, cols), BF), jax.ShapeDtypeStruct((256, cols), BF)),
         in_specs=[vmem] * 3,
         out_specs=(hbm, hbm),
-        scratch_shapes=[pltpu.VMEM((8, rows // 8, cols), BF), dma((9,))],
+        scratch_shapes=[pltpu.VMEM((4, rows, cols // 4), BF), dma((5,))],
         compiler_params=pltpu.CompilerParams(vmem_limit_bytes=32 << 20),
         name="update",
     )(current, scaled, solved.reshape(256, cols))

time: 64.9 us -> 59.5 us (0.917)
  the two profiles are of different devices: /device:TPU:32 before, /device:TPU:40 now
where the time goes in v4:
time: 59.5 us; the launch traced here: 59.4 us
  Pallas kernels  58.7 us (99%)
  between operations  0.65 us (1%)
    pallas_call x1, Pallas kernels, body(): pl.pallas_call(comm_kernel, out_shape=(jax.ShapeDtypeStruct((2, 128, cols...  56.6 us
    pallas_call x1, Pallas kernels, body(): pl.pallas_call(update_kernel, out_shape=(jax.ShapeDtypeStruct((rows, cols...  2.07 us

profile of v4, /device:TPU:40, one launch (start us, length us, event | category | flops | bytes accessed | tf_op | source)
XLA Modules:
  0.0 59.4 jit_solution(15168659858771817985)
XLA Ops:
  0.6 0.0 copy-start
  0.6 56.6 %substitute.1 = (bf16[2,128,1024]{2,1,0:T(8,128)(2,1)S(1)}, bf16[1024,256]{1,0:T(8,128)(2,1)S(1)}) custom-call(bf16[1024,1024]{1,0:T(8,128)(2,1)} %bitcast.5, bf16[1024,2,128]{2,1,0:T(2,128)(2,1)} %panel_in.1, f32[2,1024]{1,0:T(2,128)} %bitcast.8, bf16[2,128,1024]{2,1,0:T(8,128)(2,1)} %linv_in.1), custom_call_target="tpu_custom_call" | custom-call | tf_op jit(solution)/shard_map/substitute/pallas_call | solution.py:503
  57.3 0.0 copy-done
  57.3 2.1 %update.1 = (bf16[1024,1024]{1,0:T(8,128)(2,1)}, bf16[256,1024]{1,0:T(8,128)(2,1)}) custom-call(bf16[1024,1024]{1,0:T(8,128)(2,1)S(1)} %bitcast.6, bf16[1024,256]{1,0:T(8,128)(2,1)S(1)} %get-tuple-element.6.scaled, bf16[256,1024]{1,0:T(8,128)(2,1)S(1)} %bitcast.7), custom_call_target="tpu_custom_call" | custom-call | tf_op jit(solution)/shard_map/update/pallas_call | solution.py:532
Async XLA Ops:
  0.6 56.6 %copy-start = (bf16[1024,1,1024]{2,0,1:T(8,128)(2,1)S(1)}, bf16[1024,1,1024]{2,0,1:T(8,128)(2,1)}, u32[]{:S(2)}) copy-start(bf16[1024,1,1024]{2,0,1:T(8,128)(2,1)} %param.4) | copy-start | bytes 6291460

commit v5 on v4

--- a/solution.py
+++ b/solution.py
@@ -15,47 +15,54 @@
 RELAYED = (5, 7, 9, 11)
 
 
-CHILDREN = {8: (6, 5, 1), 6: (7, 0, 4), 5: (2,), 1: (3,)}
-ADDERS = ((1, 1), (0, 2), (0, 3), (3, 1))
-
-
-ORDER = ((1, 2, 3, 0), (1, 2, 3, 0))
+CHILDREN = {7: (6, 5), 0: (2,), 6: (4,), 2: (3,)}
+ADDERS = (((0, 3, 0), (0, 2, 0), (1, 1, 1), (3, 1, 0)), ((0, 3, 1), (0, 2, 1), (0, 4, 1), (2, 1, 0)))
+
+
+ORDER = ((3, 1, 2, 0), (1, 0, 2, 3))
 
 
 def place(e):
-    x = e // 2
-    return x, (0 if e % 2 == 0 else (1 if x % 2 == 0 else NZ - 1)), x // 2
-
-
-def node_place(n):
-    if n == 8:
-        return 3, 1, 0
-    x, z, core = place(n)
+    return e // 2, e % 2, e // 4
+
+
+def node_place(e):
+    x, z, core = place(e)
     return x, z, 1 - core
 
 
 def comm_kernel(
     pend, panel_in, scale_in, linv_in, out, scaled,
-    panel, scale, linv, pown, xin, part, fan, sol, prow, acc, diff, oblk,
-    ready, ld, lp, xs, xr, ps, pr, as_, ar, ls, lr, qs, qr, rs, us, ds_, dr, zs, zr_, ts, fs, fr,
+    panel, scale, linv, pown, xin, part, fan, sol, pcol, acc, sums, terms, taken, oblk,
+    ready, ld, lp, xs, xr, ps, pr, as_, ar, ls, lr, qs, qr, rs, us, bs, br, ds_, dr, es, er, zs, zr_, ts, fs, fr,
 ):
     row, col = lax.axis_index("row"), lax.axis_index("col")
     x, z = row // NZ, row % NZ
     y, h = col // 2, col % 2
     other = 2 * y + (1 - h)
-    second = jnp.where(x % 2 == 0, 1, NZ - 1)
     mine = h == x // 2
-    lead_chip = jnp.logical_or(z == 0, z == second)
+    lead_chip = z < 2
     lead = jnp.logical_and(lead_chip, mine)
     my_j = jnp.where(z == 0, 0, 1)
     my_e = jnp.where(lead, 2 * x + my_j, -1)
     source = [row == k for k in range(2)]
     my_node = jnp.where(jnp.logical_and(lead_chip, jnp.logical_not(mine)), 2 * x + my_j, -1)
-    my_node = jnp.where(jnp.logical_and(row == 3 * NZ + 1, h == 0), 8, my_node)
     my_add = jnp.int32(-1)
-    for i, (ax, az) in enumerate(ADDERS):
-        my_add = jnp.where(row == ax * NZ + az, i, my_add)
+    add_core = jnp.int32(0)
+    for hs in range(2):
+        for i, (ax, az, ac) in enumerate(ADDERS[hs]):
+            here = jnp.logical_and(row == ax * NZ + az, h == ac)
+            my_add = jnp.where(here, i, my_add)
+            add_core = jnp.where(here, hs, add_core)
+
+    def add_place(i):
+        a, b = ADDERS[0][i], ADDERS[1][i]
+        return [jnp.where(h == 0, p, q) for p, q in zip(a, b)]
+
     adder = my_add >= 0
+    before = jnp.logical_or(my_node == 0, my_node == 6)
+    behind = jnp.logical_or(my_e == 1, my_e == 7)
+    my_node = jnp.where(my_node == 1, -1, my_node)
     my_rows = pl.ds(pl.multiple_of(y * 256, 256), 256)
 
     def dev(xx, zz, cc):
@@ -110,30 +117,42 @@
             @pl.when(lead)
             def _():
                 hello((row, 2 * sy + h))
-        @pl.when(both(lead, no(source[0])) if yd == 0 else lead)
+        heads = both(lead, no(behind))
+
+        @pl.when(both(heads, no(source[0])) if yd == 0 else heads)
         def _():
             hello((0, 2 * sy + h))
 
+        @pl.when(before)
+        def _():
+            hello((0, 2 * sy + 1 - h))
+
         @pl.when(adder)
         def _():
-            hello((1, 2 * sy + h))
-
-        @pl.when(my_node == 8)
-        def _():
-            for hh in range(2):
-                hello((1, 2 * sy + hh))
+            hello((1, 2 * sy + add_core))
+
     for parent, children in CHILDREN.items():
         for child in children:
             @pl.when(my_node == child)
             def _():
                 hello(node(parent, y))
-    for i, (ax, az) in enumerate(ADDERS):
-        @pl.when(both(lead, my_e % 4 == i))
-        def _():
-            hello(dev(ax, az, col))
+    @pl.when(behind)
+    def _():
+        hello(dev(x, 0, other))
+
+    @pl.when(jnp.logical_or(my_node == 0, my_node == 7))
+    def _():
+        for hh in range(2):
+            hello((1, 2 * y + hh))
+    for i in range(4):
+        ax, az, ac = add_place(i)
+        for yd in range(NY):
+            @pl.when(both(both(lead, my_e % 4 == i), y >= yd))
+            def _():
+                hello(dev(ax, az, 2 * (y - yd) + ac))
     hello((row, other))
     lead_col = 2 * y + x // 2
-    line_z = (jnp.int32(0), second)
+    line_z = (0, 1)
     away = [(z - lz + NZ) % NZ for lz in line_z]
 
     def among(v, values):
@@ -162,8 +181,8 @@
         hello(dev((x + d) % NX, z, col))
     expect = 1 + NX - 1 + my_leads + jnp.where(lead, NY - 1, 0)
     expect += jnp.where(source[0], jnp.where(h == 0, 4 * NY - 1, 4 * NY), 0)
-    expect += jnp.where(source[1], 4 * NY + NY, 0)
-    expect += jnp.where(adder, 1, 0)
+    expect += jnp.where(source[1], 4 * NY + 2, 0)
+    expect += jnp.where(adder, NY - y, 0) + jnp.where(before, 1, 0)
     for parent, children in CHILDREN.items():
         expect += jnp.where(my_node == parent, len(children), 0)
 
@@ -180,9 +199,7 @@
                 return c
             lax.fori_loop(0, 4, scale_rows, 0)
 
-    early = jnp.logical_or(source[1], no(jnp.logical_or(source[0], lead)))
-
-    @pl.when(early)
+    @pl.when(source[1])
     def _():
         scale_panel()
 
@@ -205,33 +222,54 @@
         return remote(pend.at[:, lanes(4 * (1 - h) + i)], xin.at[i], xs.at[i], xr.at[i], (row, other))
 
     def scatter_copy(k, i, yd):
-        zz = 0 if i % 2 == 0 else (1 if i // 2 == 0 else NZ - 1)
-        tx = 2 * h + i // 2
+        tx, tz, core = 2 * h + i // 2, (0, h, 0, 1 - h)[i], (h, 1, h, 0)[i]
         if k == 1:
-            tx, zz = ADDERS[i]
+            tx, tz, core = add_place(i)
         ty = (y + yd) % NY
         rows = pl.ds(pl.multiple_of(ty * 256, 256), 256)
         return remote(xin.at[i, rows], part.at[k, yd], ps.at[i, yd], pr.at[k, yd],
-                      dev(tx, zz, 2 * ty + h))
-
-    def panel_copy(yd):
-        ty = (y + yd) % NY
-        rows = pl.ds(pl.multiple_of(ty * 256, 256), 256)
-        return remote(scaled.at[rows, pl.ds(0, 128)], prow.at[:, lanes(col)], qs.at[yd], qr.at[col],
-                      node(8, ty))
-
-    def panel_wait(c):
-        return remote(prow.at[:, lanes(c)], prow.at[:, lanes(c)], qs.at[0], qr.at[c], (row, other))
-
-    def relay_copy(child, n, c):
-        return remote(prow.at[:, lanes(c)], prow.at[:, lanes(c)], rs.at[n, c], qr.at[c], node(child, y))
-
-    def mate_copy(c):
-        return remote(prow.at[:, lanes(c)], prow.at[:, lanes(c)], us.at[c], qr.at[c], (row, other))
-
-    def diff_copy(i):
-        tz = 0 if i % 2 == 0 else (1 if i // 2 == 0 else NZ - 1)
-        return remote(acc, diff, ds_, dr, dev(2 * h + i // 2, tz, col))
+                      dev(tx, tz, 2 * ty + core))
+
+    def before_copy():
+        return remote(acc, fan.at[0, my_rows], bs, br, dev(x, 1, other))
+
+    def before_wait():
+        return remote(acc, fan.at[0, my_rows], bs, br, dev(x, 0, other))
+
+    def panel_block(q):
+        return pcol.at[pl.ds((q % 4) * 256, 256), pl.ds((q // 4) * 128, 128)]
+
+    def panel_copy(t, r):
+        rows = pl.ds(r * 256, 256)
+        target = (node(0, y), (row, other), node(7, y))[t]
+        return remote(scaled.at[rows, pl.ds(0, 128)], pcol.at[rows, lanes(h)],
+                      qs.at[t, r], qr.at[4 * h + r], target)
+
+    def panel_wait(q):
+        return remote(panel_block(q), panel_block(q), qs.at[0, 0], qr.at[q], (row, other))
+
+    def relay_copy(child, n, q):
+        return remote(panel_block(q), panel_block(q), rs.at[n, q], qr.at[q], node(child, y))
+
+    def mate_copy(q):
+        return remote(panel_block(q), panel_block(q), us.at[q], qr.at[q], (row, other))
+
+    def sums_copy(i, yd):
+        tz = i % 2
+        return remote(acc, sums.at[my_rows], ds_.at[yd], dr.at[y],
+                      dev(2 * add_core + i // 2, tz, 2 * (y + yd) + add_core))
+
+    def sums_wait(sy):
+        rows = sums.at[pl.ds(sy * 256, 256)]
+        return remote(rows, rows, ds_.at[0], dr.at[sy], (row, other))
+
+    def terms_copy(t):
+        rows = pl.ds(0, (t + 1) * 256)
+        return remote(terms.at[rows], taken.at[y, rows], es.at[t], er.at[y], (row, 2 * t + h))
+
+    def terms_wait(t, sy):
+        rows = taken.at[sy, pl.ds(0, (t + 1) * 256)]
+        return remote(rows, rows, es.at[t], er.at[sy], (row, other))
 
     def gather_copy(buf, n, yd):
         return remote(buf.at[my_rows], buf.at[my_rows], as_.at[n, yd - 1], ar.at[n, yd - 1],
@@ -294,8 +332,18 @@
 
     @pl.when(source[1])
     def _():
-        for yd in range(NY):
-            panel_copy(yd).start()
+        for r in range(4):
+            panel_copy(0, r).start()
+            panel_copy(2, r).start()
+
+        @pl.when(h == 0)
+        def _():
+            pcol[:, 0:128] = scaled[:, 0:128]
+
+        @pl.when(h == 1)
+        def _():
+            for r in range(4):
+                panel_copy(1, r).start()
 
     for k in range(2):
         @pl.when(source[k])
@@ -319,7 +367,7 @@
         if k == 1:
             scatter_copy(k, 0, 0).wait_recv()
         else:
-            @pl.when(no(source[0]))
+            @pl.when(my_e != 0)
             def _():
                 scatter_copy(k, 0, 0).wait_recv()
         for yd in range(1, NY):
@@ -337,8 +385,8 @@
         for yd in range(1, NY):
             gather_copy(buf, n, yd).wait_recv()
 
-    def solve(k):
-        blocks = jnp.dot(linv[k], fan[k], preferred_element_type=F32).astype(BF)
+    def solve(k, depth):
+        blocks = jnp.dot(linv[k, :, :depth], fan[k, :depth], preferred_element_type=F32).astype(BF)
         oblk[k] = blocks[128:]
         out[k, :, lanes(2 * x + my_j)] = blocks[:128]
         return blocks
@@ -355,15 +403,21 @@
     def add_up():
         @pl.when(adder)
         def _():
-            acc[...] = reduced(1)
+            acc[...] = reduced(1).astype(BF)
             for i in range(4):
-                @pl.when(my_add == i)
-                def _():
-                    diff_copy(i).start()
+                for yd in (2, 1, 3, 0):
+                    @pl.when(both(my_add == i, y + yd < NY))
+                    def _():
+                        sums_copy(i, yd).start()
+
+    @pl.when(before)
+    def _():
+        acc[...] = reduced(0).astype(BF)
+        before_copy().start()
 
     @pl.when(my_node >= 0)
     def _():
-        for c in range(8):
+        for c in (0, 4, 1, 5, 2, 6, 3, 7):
             panel_wait(c).wait_recv()
             for parent, children in CHILDREN.items():
                 @pl.when(my_node == parent)
@@ -371,42 +425,65 @@
                     for n, child in enumerate(children):
                         relay_copy(child, n, c).start()
 
-            @pl.when(my_node != 8)
-            def _():
-                mate_copy(c).start()
+            mate_copy(c).start()
 
     @pl.when(lead)
     def _():
-        fan[0, my_rows] = reduced(0).astype(BF)
+        @pl.when(behind)
+        def _():
+            before_wait().wait_recv()
+
+        @pl.when(no(behind))
+        def _():
+            fan[0, my_rows] = reduced(0).astype(BF)
         gather_start(fan.at[0], 0)
         for k in range(2):
             linv_copy(k).wait_recv()
         load(2).wait()
         gather_wait(fan.at[0], 0)
-        blocks = solve(0)
-        sol[pl.ds(pl.multiple_of(col * 128, 128), 128)] = blocks[:128]
-        sol[pl.ds(pl.multiple_of(other * 128, 128), 128)] = blocks[128:]
-        gather_start(sol, 1)
+        blocks = solve(0, fan.shape[1])
+        sol[pl.ds(pl.multiple_of(h * 128, 128), 128)] = blocks[:128]
+        sol[pl.ds(pl.multiple_of((1 - h) * 128, 128), 128)] = blocks[128:]
+        for q in range(8):
+            if q < 4:
+                @pl.when(my_e != 1)
+                def _():
+                    panel_wait(q).wait_recv()
+            else:
+                panel_wait(q).wait_recv()
+        terms[...] = jnp.dot(pcol[...], sol[...], preferred_element_type=F32).astype(BF)
+        for t in (3, 2, 1, 0):
+            @pl.when(y != t)
+            def _():
+                terms_copy(t).start()
         pl.semaphore_wait(ready, 2 * len(DIRECT))
         line_start(0)
-        diff_copy(0).wait_recv()
-        for c in range(8):
-            panel_wait(c).wait_recv()
-        gather_wait(sol, 1)
-        fan[1, my_rows] = (
-            diff[...] - jnp.dot(prow[...], sol[...], preferred_element_type=F32)).astype(BF)
-        gather_start(fan.at[1], 2)
         spread(0)
-        gather_wait(fan.at[1], 2)
-        solve(1)
+        for t in range(NY):
+            @pl.when(y == t)
+            def _():
+                depth = (t + 1) * 256
+                for sy in range(t + 1):
+                    sums_wait(sy).wait_recv()
+                total = sums[:depth].astype(F32) - terms[:depth].astype(F32)
+                for sy in range(NY):
+                    if sy != t:
+                        terms_wait(t, sy).wait_recv()
+                        total -= taken[sy, :depth].astype(F32)
+                fan[1, :depth] = total.astype(BF)
+                solve(1, depth)
         line_start(1)
 
     @pl.when(no(lead))
     def _():
         add_up()
+
+        @pl.when(no(source[1]))
+        def _():
+            scale_panel()
         spread(0)
 
-    @pl.when(no(early))
+    @pl.when(both(lead, no(source[1])))
     def _():
         scale_panel()
     spread(1)
@@ -441,22 +518,38 @@
 
     @pl.when(source[1])
     def _():
-        for yd in range(NY):
-            panel_copy(yd).wait_send()
+        for r in range(4):
+            panel_copy(0, r).wait_send()
+            panel_copy(2, r).wait_send()
+
+        @pl.when(h == 1)
+        def _():
+            for r in range(4):
+                panel_copy(1, r).wait_send()
 
     @pl.when(lead)
     def _():
-        for n, buf in enumerate((fan.at[0], sol, fan.at[1])):
-            for yd in range(1, NY):
-                gather_copy(buf, n, yd).wait_send()
+        for yd in range(1, NY):
+            gather_copy(fan.at[0], 0, yd).wait_send()
+        for t in range(NY):
+            @pl.when(y != t)
+            def _():
+                terms_copy(t).wait_send()
         for k in range(2):
             for d in DIRECT:
                 line_copy(k, 0, d, False).wait_send()
                 line_copy(k, 0, d, True).wait_send()
             line_copy(k, 0, 0, False).wait_send()
+    @pl.when(before)
+    def _():
+        before_copy().wait_send()
+
     @pl.when(adder)
     def _():
-        diff_copy(0).wait_send()
+        for yd in range(NY):
+            @pl.when(y + yd < NY)
+            def _():
+                sums_copy(0, yd).wait_send()
 
     @pl.when(my_node >= 0)
     def _():
@@ -467,9 +560,7 @@
                     for n, child in enumerate(children):
                         relay_copy(child, n, c).wait_send()
 
-            @pl.when(my_node != 8)
-            def _():
-                mate_copy(c).wait_send()
+            mate_copy(c).wait_send()
 
 
 def update_kernel(pend, scaled, solved, out, solved_out, done, sem):
@@ -513,15 +604,18 @@
             pltpu.VMEM((4, rows, 128), BF),
             pltpu.VMEM((2, NY, 256, 128), BF),
             pltpu.VMEM((2, rows, 128), BF),
+            pltpu.VMEM((256, 128), BF),
+            pltpu.VMEM((rows, 256), BF),
+            pltpu.VMEM((256, 128), BF),
             pltpu.VMEM((rows, 128), BF),
-            pltpu.VMEM((256, rows), BF),
-            pltpu.VMEM((256, 128), F32),
-            pltpu.VMEM((256, 128), F32),
+            pltpu.VMEM((rows, 128), BF),
+            pltpu.VMEM((NY, rows, 128), BF),
             pltpu.VMEM((2, 128, 128), BF),
             pltpu.SemaphoreType.REGULAR, dma((3,)), dma((4,)),
             dma((4,)), dma((4,)), dma((4, NY)), dma((2, NY)),
-            dma((3, NY - 1)), dma((3, NY - 1)), dma((2,)), dma((2,)),
-            dma((NY,)), dma((8,)), dma((3, 8)), dma((8,)), dma, dma,
+            dma((1, NY - 1)), dma((1, NY - 1)), dma((2,)), dma((2,)),
+            dma((3, 4)), dma((8,)), dma((2, 8)), dma((8,)), dma, dma, dma((NY,)), dma((NY,)),
+            dma((NY,)), dma((NY,)),
             dma((2, NZ, 2)), dma((2, 2)), dma((2, 2)), dma((2, 2, NX - 1)), dma((2, 2, NX - 1)),
         ],
         compiler_params=pltpu.CompilerParams(

time: 59.5 us -> 54.1 us (0.909)
  the two profiles are of different devices: /device:TPU:40 before, /device:TPU:34 now
where the time goes in v5:
time: 54.1 us; the launch traced here: 54 us
  Pallas kernels  53.3 us (99%)
  between operations  0.65 us (1%)
    pallas_call x1, Pallas kernels, body(): pl.pallas_call(comm_kernel, out_shape=(jax.ShapeDtypeStruct((2, 128, cols...  51.3 us
    pallas_call x1, Pallas kernels, body(): pl.pallas_call(update_kernel, out_shape=(jax.ShapeDtypeStruct((rows, cols...  2.06 us

profile of v5, /device:TPU:34, one launch (start us, length us, event | category | flops | bytes accessed | tf_op | source)
XLA Modules:
  0.0 54.0 jit_solution(1408929249167494753)
XLA Ops:
  0.6 0.0 copy-start
  0.6 51.3 %substitute.1 = (bf16[2,128,1024]{2,1,0:T(8,128)(2,1)S(1)}, bf16[1024,256]{1,0:T(8,128)(2,1)S(1)}) custom-call(bf16[1024,1024]{1,0:T(8,128)(2,1)} %bitcast.5, bf16[1024,2,128]{2,1,0:T(2,128)(2,1)} %panel_in.1, f32[2,1024]{1,0:T(2,128)} %bitcast.8, bf16[2,128,1024]{2,1,0:T(8,128)(2,1)} %linv_in.1), custom_call_target="tpu_custom_call" | custom-call | tf_op jit(solution)/shard_map/substitute/pallas_call | solution.py:594
  51.9 0.0 copy-done
  51.9 2.1 %update.1 = (bf16[1024,1024]{1,0:T(8,128)(2,1)}, bf16[256,1024]{1,0:T(8,128)(2,1)}) custom-call(bf16[1024,1024]{1,0:T(8,128)(2,1)S(1)} %bitcast.6, bf16[1024,256]{1,0:T(8,128)(2,1)S(1)} %get-tuple-element.6.scaled, bf16[256,1024]{1,0:T(8,128)(2,1)S(1)} %bitcast.7), custom_call_target="tpu_custom_call" | custom-call | tf_op jit(solution)/shard_map/update/pallas_call | solution.py:626
Async XLA Ops:
  0.6 51.3 %copy-start = (bf16[1024,1,1024]{2,0,1:T(8,128)(2,1)S(1)}, bf16[1024,1,1024]{2,0,1:T(8,128)(2,1)}, u32[]{:S(2)}) copy-start(bf16[1024,1,1024]{2,0,1:T(8,128)(2,1)} %param.4) | copy-start | bytes 6291460

commit v6 on v5

--- a/solution.py
+++ b/solution.py
@@ -16,10 +16,10 @@
 
 
 CHILDREN = {7: (6, 5), 0: (2,), 6: (4,), 2: (3,)}
-ADDERS = (((0, 3, 0), (0, 2, 0), (1, 1, 1), (3, 1, 0)), ((0, 3, 1), (0, 2, 1), (0, 4, 1), (2, 1, 0)))
-
-
-ORDER = ((3, 1, 2, 0), (1, 0, 2, 3))
+ADDERS = (((1, 2, 0), (0, 2, 0), (3, 1, 0), (1, 1, 1)), ((3, 2, 1), (0, 2, 1), (1, 2, 1), (2, 1, 0)))
+
+
+ORDER = ((3, 1, 2, 0), (0, 2, 1, 3))
 
 
 def place(e):
@@ -400,8 +400,8 @@
                     line_copy(k, j, d, True).start()
                 line_copy(k, j, 0, False).start()
 
-    def add_up():
-        @pl.when(adder)
+    def add_up(which):
+        @pl.when(both(adder, which))
         def _():
             acc[...] = reduced(1).astype(BF)
             for i in range(4):
@@ -414,6 +414,8 @@
     def _():
         acc[...] = reduced(0).astype(BF)
         before_copy().start()
+
+    add_up(my_node != 7)
 
     @pl.when(my_node >= 0)
     def _():
@@ -476,7 +478,7 @@
 
     @pl.when(no(lead))
     def _():
-        add_up()
+        add_up(my_node == 7)
 
         @pl.when(no(source[1]))
         def _():

time: 54.1 us -> 53.5 us (0.989)
  the two profiles are of different devices: /device:TPU:34 before, /device:TPU:408 now
where the time goes in v6:
time: 53.5 us; the launch traced here: 53.3 us
  Pallas kernels  52.7 us (99%)
  between operations  0.65 us (1%)
    pallas_call x1, Pallas kernels, body(): pl.pallas_call(comm_kernel, out_shape=(jax.ShapeDtypeStruct((2, 128, cols...  50.6 us
    pallas_call x1, Pallas kernels, body(): pl.pallas_call(update_kernel, out_shape=(jax.ShapeDtypeStruct((rows, cols...  2.08 us

profile of v6, /device:TPU:408, one launch (start us, length us, event | category | flops | bytes accessed | tf_op | source)
XLA Modules:
  0.0 53.3 jit_solution(16665219751117205045)
XLA Ops:
  0.6 0.0 copy-start
  0.6 50.6 %substitute.1 = (bf16[2,128,1024]{2,1,0:T(8,128)(2,1)S(1)}, bf16[1024,256]{1,0:T(8,128)(2,1)S(1)}) custom-call(bf16[1024,1024]{1,0:T(8,128)(2,1)} %bitcast.5, bf16[1024,2,128]{2,1,0:T(2,128)(2,1)} %panel_in.1, f32[2,1024]{1,0:T(2,128)} %bitcast.8, bf16[2,128,1024]{2,1,0:T(8,128)(2,1)} %linv_in.1), custom_call_target="tpu_custom_call" | custom-call | tf_op jit(solution)/shard_map/substitute/pallas_call | solution.py:596
  51.3 0.0 copy-done
  51.3 2.1 %update.1 = (bf16[1024,1024]{1,0:T(8,128)(2,1)}, bf16[256,1024]{1,0:T(8,128)(2,1)}) custom-call(bf16[1024,1024]{1,0:T(8,128)(2,1)S(1)} %bitcast.6, bf16[1024,256]{1,0:T(8,128)(2,1)S(1)} %get-tuple-element.6.scaled, bf16[256,1024]{1,0:T(8,128)(2,1)S(1)} %bitcast.7), custom_call_target="tpu_custom_call" | custom-call | tf_op jit(solution)/shard_map/update/pallas_call | solution.py:628
Async XLA Ops:
  0.6 50.6 %copy-start = (bf16[1024,1,1024]{2,0,1:T(8,128)(2,1)S(1)}, bf16[1024,1,1024]{2,0,1:T(8,128)(2,1)}, u32[]{:S(2)}) copy-start(bf16[1024,1,1024]{2,0,1:T(8,128)(2,1)} %param.4) | copy-start | bytes 6291460

commit v7 on v6

--- a/solution.py
+++ b/solution.py
@@ -11,7 +11,7 @@
 NX, NY, NZ = 4, 4, 16
 BF = jnp.bfloat16
 F32 = jnp.float32
-DIRECT = (6, 10, 8, 4, 12, 3, 13, 2, 14, 1, 15)
+DIRECT = (6, 10, 4, 12, 3, 13, 2, 14, 1, 15, 8)
 RELAYED = (5, 7, 9, 11)
 
 

time: 53.5 us -> 52.1 us (0.974)
  Pallas kernels: 52.7 us -> 51.3 us
    pallas_call x1, Pallas kernels: 50.6 us -> 49.3 us  [body(): pl.pallas_call(comm_kernel, out_shape=(jax.ShapeDtypeStruct((2, 128, cols...]
where the time goes in v7:
time: 52.1 us; the launch traced here: 52 us
  Pallas kernels  51.3 us (98%)
  between operations  0.65 us (1%)
    pallas_call x1, Pallas kernels, body(): pl.pallas_call(comm_kernel, out_shape=(jax.ShapeDtypeStruct((2, 128, cols...  49.3 us
    pallas_call x1, Pallas kernels, body(): pl.pallas_call(update_kernel, out_shape=(jax.ShapeDtypeStruct((rows, cols...  2.06 us

profile of v7, /device:TPU:408, one launch (start us, length us, event | category | flops | bytes accessed | tf_op | source)
XLA Modules:
  0.0 52.0 jit_solution(13412797299547089153)
XLA Ops:
  0.6 0.0 copy-start
  0.6 49.3 %substitute.1 = (bf16[2,128,1024]{2,1,0:T(8,128)(2,1)S(1)}, bf16[1024,256]{1,0:T(8,128)(2,1)S(1)}) custom-call(bf16[1024,1024]{1,0:T(8,128)(2,1)} %bitcast.5, bf16[1024,2,128]{2,1,0:T(2,128)(2,1)} %panel_in.1, f32[2,1024]{1,0:T(2,128)} %bitcast.8, bf16[2,128,1024]{2,1,0:T(8,128)(2,1)} %linv_in.1), custom_call_target="tpu_custom_call" | custom-call | tf_op jit(solution)/shard_map/substitute/pallas_call | solution.py:596
  49.9 0.0 copy-done
  49.9 2.1 %update.1 = (bf16[1024,1024]{1,0:T(8,128)(2,1)}, bf16[256,1024]{1,0:T(8,128)(2,1)}) custom-call(bf16[1024,1024]{1,0:T(8,128)(2,1)S(1)} %bitcast.6, bf16[1024,256]{1,0:T(8,128)(2,1)S(1)} %get-tuple-element.6.scaled, bf16[256,1024]{1,0:T(8,128)(2,1)S(1)} %bitcast.7), custom_call_target="tpu_custom_call" | custom-call | tf_op jit(solution)/shard_map/update/pallas_call | solution.py:628
Async XLA Ops:
  0.6 49.3 %copy-start = (bf16[1024,1,1024]{2,0,1:T(8,128)(2,1)S(1)}, bf16[1024,1,1024]{2,0,1:T(8,128)(2,1)}, u32[]{:S(2)}) copy-start(bf16[1024,1,1024]{2,0,1:T(8,128)(2,1)} %param.4) | copy-start | bytes 6291460
